TPU v7x, 32 devices: a whole 2x2x4 slice. The times are simulated.
32 devices in a mesh: seq: 4 (over y, core), ctx: 8 (over z, x).
Axes of the slice: x: 2, y: 2, z: 4, core: 2. Of those that a mesh axis runs over, the one named last changes fastest.
Arguments:
- tokens: bfloat16 [4, 1024, 2048], P('seq', 'ctx'), may hold values from -6 to 6
- cotangent: bfloat16 [4, 1024, 2048], P('seq', 'ctx'), may hold values from -6 to 6
- gain_attn: bfloat16 [2048], P(('seq', 'ctx')), may hold values from 0.099609375 to 1.8984375
- w_query: bfloat16 [2048, 2048], P(('seq', 'ctx')), may hold values from -0.125 to 0.125
- w_key: bfloat16 [2048, 1024], P(('seq', 'ctx')), may hold values from -0.125 to 0.125
- w_value: bfloat16 [2048, 1024], P(('seq', 'ctx')), may hold values from -0.125 to 0.125
- w_out: bfloat16 [2048, 2048], P(('seq', 'ctx')), may hold values from -1 to 1
- gain_mlp: bfloat16 [2048], P(('seq', 'ctx')), may hold values from 0.099609375 to 1.8984375
- w_gate: bfloat16 [2048, 8192], P(('seq', 'ctx')), may hold values from -0.125 to 0.125
- w_up: bfloat16 [2048, 8192], P(('seq', 'ctx')), may hold values from -0.125 to 0.125
- w_down: bfloat16 [8192, 2048], P(('seq', 'ctx')), may hold values from -0.0625 to 0.0625
- pair_order: int32 [4, 8], P('seq'), may hold values from 0 to 7, each once within a row
- segments: int32 [4, 1024], P('seq'), may hold values from 0 to 3, never falling along the last dimension, each value on 1 to 512 neighbouring positions
Outputs:
- output: bfloat16 [4, 1024, 2048], P('seq', 'ctx')
- grad_tokens: float32 [4, 1024, 2048], P('seq', 'ctx')
- grad_gain_attn: float32 [2048], P(('seq', 'ctx'))
- grad_w_query: float32 [2048, 2048], P(('seq', 'ctx'))
- grad_w_key: float32 [2048, 1024], P(('seq', 'ctx'))
- grad_w_value: float32 [2048, 1024], P(('seq', 'ctx'))
- grad_w_out: float32 [2048, 2048], P(('seq', 'ctx'))
- grad_gain_mlp: float32 [2048], P(('seq', 'ctx'))
- grad_w_gate: float32 [2048, 8192], P(('seq', 'ctx'))
- grad_w_up: float32 [2048, 8192], P(('seq', 'ctx'))
- grad_w_down: float32 [8192, 2048], P(('seq', 'ctx'))
Inputs may be any that keep to these rules, and one draw needn't show every extreme that they name: `segments`: along a sequence the document numbers never fall; each document has 1 to 512 tokens. `pair_order`: each row holds every number of 0 to 7 once.
All inputs are finite; a program needn't handle non-finite values.
Results may differ from a plain program's by a relative error of at most 0.022.
Values may be sent and summed in bfloat16 or wider, within the bound.
A program may use at most 448 MiB of HBM per device.

v0:
```python
import math

import jax
import jax.numpy as jnp
from jax import lax
from jax.sharding import PartitionSpec as P

H = 8
KVH = 4
HDIM = 256


EPSILON = 1e-06
THETA = 1000042.0
NEG_FILL = -1e30


def slot_positions(pair_row, half_rows, pair_count):
    offsets = jnp.arange(half_rows, dtype=jnp.int32)
    low_slots = pair_row[:, None] * half_rows + offsets[None, :]
    high_slots = (2 * pair_count - 1 - pair_row)[:, None] * half_rows + offsets[None, :]
    return jnp.concatenate([low_slots, high_slots], axis=1).reshape(-1)


def rotary_tables(positions, head_dim):
    half_dim = head_dim // 2
    frequency = THETA ** (-(jnp.arange(half_dim, dtype=jnp.float32) * 2.0 / head_dim))
    angles = positions.astype(jnp.float32)[:, None] * frequency[None, :]
    return (jnp.cos(angles)[:, None, :], jnp.sin(angles)[:, None, :])


def rotary(tensor, table_cos, table_sin):
    half_dim = tensor.shape[-1] // 2
    lead_half = tensor[..., :half_dim]
    tail_half = tensor[..., half_dim:]
    return jnp.concatenate(
        [
            lead_half * table_cos - tail_half * table_sin,
            tail_half * table_cos + lead_half * table_sin,
        ],
        axis=-1,
    )


def rms_scale(tensor):
    return lax.rsqrt(jnp.mean(tensor * tensor, axis=-1, keepdims=True) + EPSILON)


def rms_backward(tensor, scale_rows, gain_full, grad_rows):
    weighted = gain_full * grad_rows
    inner_mean = jnp.mean(weighted * tensor, axis=-1, keepdims=True)
    return scale_rows * weighted - tensor * (scale_rows * scale_rows * scale_rows) * inner_mean


def contract_rows(first_mat, second_mat):
    return lax.dot_general(
        first_mat, second_mat, (((0,), (0,)), ((), ())), preferred_element_type=jnp.float32
    )


def contract_cols(first_mat, second_mat):
    return lax.dot_general(
        first_mat, second_mat, (((1,), (1,)), ((), ())), preferred_element_type=jnp.float32
    )


def attention_weights(gain_attn, gain_mlp, w_query, w_key, w_value, w_out):
    return (
        lax.all_gather(gain_attn, ("seq", "ctx"), axis=0, tiled=True),
        lax.all_gather(gain_mlp, ("seq", "ctx"), axis=0, tiled=True),
        lax.all_gather(w_query, ("seq", "ctx"), axis=0, tiled=True),
        lax.all_gather(w_key, ("seq", "ctx"), axis=0, tiled=True),
        lax.all_gather(w_value, ("seq", "ctx"), axis=0, tiled=True),
        lax.all_gather(w_out, ("seq", "ctx"), axis=0, tiled=True),
    )


def mlp_weights(w_gate, w_up, w_down):
    return (
        lax.all_gather(w_gate, ("seq", "ctx"), axis=0, tiled=True),
        lax.all_gather(w_up, ("seq", "ctx"), axis=0, tiled=True),
        lax.all_gather(w_down, ("seq", "ctx"), axis=0, tiled=True),
    )


def reduce_grads(grad_one, grad_two, grad_three):
    seq_count = lax.axis_size("seq")
    grad_one = grad_one.reshape((seq_count, grad_one.shape[0] // seq_count) + grad_one.shape[1:])
    grad_two = grad_two.reshape((seq_count, grad_two.shape[0] // seq_count) + grad_two.shape[1:])
    grad_three = grad_three.reshape(
        (seq_count, grad_three.shape[0] // seq_count) + grad_three.shape[1:]
    )
    grad_one, grad_two, grad_three = (
        lax.psum_scatter(
            grad_one.astype(jnp.bfloat16), "ctx", scatter_dimension=1, tiled=True
        ).astype(jnp.float32),
        lax.psum_scatter(
            grad_two.astype(jnp.bfloat16), "ctx", scatter_dimension=1, tiled=True
        ).astype(jnp.float32),
        lax.psum_scatter(
            grad_three.astype(jnp.bfloat16), "ctx", scatter_dimension=1, tiled=True
        ).astype(jnp.float32),
    )
    grad_one, grad_two, grad_three = (
        lax.psum_scatter(
            grad_one.astype(jnp.bfloat16), "seq", scatter_dimension=0, tiled=True
        ).astype(jnp.float32),
        lax.psum_scatter(
            grad_two.astype(jnp.bfloat16), "seq", scatter_dimension=0, tiled=True
        ).astype(jnp.float32),
        lax.psum_scatter(
            grad_three.astype(jnp.bfloat16), "seq", scatter_dimension=0, tiled=True
        ).astype(jnp.float32),
    )
    return (grad_one[0], grad_two[0], grad_three[0])


def per_device(
    tokens,
    cotangent,
    gain_attn,
    w_query,
    w_key,
    w_value,
    w_out,
    gain_mlp,
    w_gate,
    w_up,
    w_down,
    pair_order,
    segments,
):
    pair_count = lax.axis_size("ctx")
    my_index = lax.axis_index("ctx")
    row_count = tokens.shape[1]
    half_rows = row_count // 2
    seq_len = segments.shape[1]
    head_groups = H // KVH
    score_scale = HDIM ** (-0.5)
    key_rows = math.gcd(seq_len, 512)
    key_steps = seq_len // key_rows
    key_pos = slot_positions(pair_order[0], half_rows, pair_count)
    key_doc = jnp.take(segments[0], key_pos)
    query_pos = lax.dynamic_slice_in_dim(key_pos, my_index * row_count, row_count)
    query_doc = lax.dynamic_slice_in_dim(key_doc, my_index * row_count, row_count)
    rot_cos, rot_sin = rotary_tables(query_pos, HDIM)
    gain_one, gain_two, query_w, key_w, value_w, out_w = attention_weights(
        gain_attn, gain_mlp, w_query, w_key, w_value, w_out
    )
    gain_one = gain_one.astype(jnp.float32)
    gain_two = gain_two.astype(jnp.float32)
    inputs = tokens[0].astype(jnp.float32)
    scale_one = rms_scale(inputs)
    normed = (inputs * scale_one * gain_one).astype(jnp.bfloat16)
    query_proj = jnp.dot(normed, query_w, preferred_element_type=jnp.float32).reshape(
        row_count, H, HDIM
    )
    key_proj = jnp.dot(normed, key_w, preferred_element_type=jnp.float32).reshape(
        row_count, KVH, HDIM
    )
    value_proj = jnp.dot(normed, value_w, preferred_element_type=jnp.float32)
    query_rot = (
        rotary(query_proj, rot_cos, rot_sin)
        .astype(jnp.bfloat16)
        .reshape(row_count, KVH, head_groups, HDIM)
    )
    key_rot = rotary(key_proj, rot_cos, rot_sin).astype(jnp.bfloat16).reshape(row_count, KVH * HDIM)
    value_low = value_proj.astype(jnp.bfloat16)
    key_width = key_rot.shape[1]
    key_all, value_all = (
        lax.all_gather(key_rot, "ctx", axis=0, tiled=True),
        lax.all_gather(value_low, "ctx", axis=0, tiled=True),
    )
    pos_blocks = key_pos.reshape(key_steps, key_rows)
    doc_blocks = key_doc.reshape(key_steps, key_rows)

    def scores_of(key_blk, pos_blk, doc_blk):
        key_heads = key_blk.reshape(key_rows, KVH, HDIM)
        raw_scores = (
            jnp.einsum("qkgd,tkd->kgqt", query_rot, key_heads, preferred_element_type=jnp.float32)
            * score_scale
        )
        visible = (doc_blk[None, :] == query_doc[:, None]) & (
            pos_blk[None, :] <= query_pos[:, None]
        )
        return (raw_scores, visible[None, None])

    def first_pass(carried, step_data):
        running_top, running_sum = carried
        key_blk, pos_blk, doc_blk = step_data
        raw_scores, visible = scores_of(key_blk, pos_blk, doc_blk)
        masked = jnp.where(visible, raw_scores, NEG_FILL)
        new_top = jnp.maximum(running_top, jnp.max(masked, axis=-1))
        added = jnp.sum(jnp.where(visible, jnp.exp(masked - new_top[..., None]), 0.0), axis=-1)
        return ((new_top, running_sum * jnp.exp(running_top - new_top) + added), None)

    start_top = jnp.full((KVH, head_groups, row_count), NEG_FILL, jnp.float32)
    start_sum = jnp.zeros((KVH, head_groups, row_count), jnp.float32)
    key_stack = key_all.reshape(key_steps, key_rows, key_width)
    value_stack = value_all.reshape(key_steps, key_rows, key_width)
    (final_top, final_sum), _ = lax.scan(
        first_pass, (start_top, start_sum), (key_stack, pos_blocks, doc_blocks)
    )
    log_total = final_top + jnp.log(final_sum)

    def second_pass(carried, step_data):
        acc_out, acc_rest = carried
        key_blk, value_blk, pos_blk, doc_blk = step_data
        raw_scores, visible = scores_of(key_blk, pos_blk, doc_blk)
        prob_full = jnp.where(visible, jnp.exp(raw_scores - log_total[..., None]), 0.0)
        prob_low = prob_full.astype(jnp.bfloat16)
        prob_rest = (prob_full - prob_low.astype(jnp.float32)).astype(jnp.bfloat16)
        value_heads = value_blk.reshape(key_rows, KVH, HDIM)
        acc_out = acc_out + jnp.einsum(
            "kgqt,tkd->qkgd", prob_low, value_heads, preferred_element_type=jnp.float32
        )
        acc_rest = acc_rest + jnp.einsum(
            "kgqt,tkd->qkgd", prob_rest, value_heads, preferred_element_type=jnp.float32
        )
        return ((acc_out, acc_rest), None)

    start_acc = jnp.zeros((row_count, KVH, head_groups, HDIM), jnp.float32)
    (attended, attended_rest), _ = lax.scan(
        second_pass, (start_acc, start_acc), (key_stack, value_stack, pos_blocks, doc_blocks)
    )
    exact_out = attended + attended_rest
    out_low = attended.reshape(row_count, H * HDIM).astype(jnp.bfloat16)
    hidden = inputs + jnp.dot(out_low, out_w, preferred_element_type=jnp.float32)
    scale_two = rms_scale(hidden)
    normed_two = (hidden * scale_two * gain_two).astype(jnp.bfloat16)
    grad_out = cotangent[0]
    gate_w, up_w, down_w = mlp_weights(w_gate, w_up, w_down)
    gate_proj = jnp.dot(normed_two, gate_w, preferred_element_type=jnp.float32)
    up_proj = jnp.dot(normed_two, up_w, preferred_element_type=jnp.float32)
    gate_sig = jax.nn.sigmoid(gate_proj)
    active = gate_proj * gate_sig
    middle = (active * up_proj).astype(jnp.bfloat16)
    result = hidden + jnp.dot(middle, down_w, preferred_element_type=jnp.float32)
    output = result.astype(jnp.bfloat16)[None]
    gate_w, up_w, down_w = mlp_weights(w_gate, w_up, w_down)
    grad_mid = contract_cols(grad_out, down_w)
    grad_gate = (grad_mid * up_proj * gate_sig * (1.0 + gate_proj * (1.0 - gate_sig))).astype(
        jnp.bfloat16
    )
    grad_up = (grad_mid * active).astype(jnp.bfloat16)
    grad_norm_two = contract_cols(grad_gate, gate_w) + contract_cols(grad_up, up_w)
    grad_gain_two = jnp.sum(grad_norm_two * hidden * scale_two, axis=0)
    grad_hidden = grad_out.astype(jnp.float32) + rms_backward(
        hidden, scale_two, gain_two, grad_norm_two
    )
    grad_w_gate = contract_rows(normed_two, grad_gate)
    grad_w_up = contract_rows(normed_two, grad_up)
    shard_gain_two, shard_gate, shard_up = reduce_grads(grad_gain_two, grad_w_gate, grad_w_up)
    gain_one, gain_two, query_w, key_w, value_w, out_w = attention_weights(
        gain_attn, gain_mlp, w_query, w_key, w_value, w_out
    )
    gain_one = gain_one.astype(jnp.float32)
    grad_branch = grad_hidden.astype(jnp.bfloat16)
    grad_w_out = contract_rows(out_low, grad_branch)
    grad_att = (
        contract_cols(grad_branch, out_w)
        .astype(jnp.bfloat16)
        .reshape(row_count, KVH, head_groups, HDIM)
    )
    row_delta = jnp.transpose(jnp.sum(grad_att.astype(jnp.float32) * exact_out, axis=-1), (1, 2, 0))
    key_back, value_back = (key_all, value_all)

    def backward_step(grad_query, step_data):
        key_blk, value_blk, pos_blk, doc_blk = step_data
        raw_scores, visible = scores_of(key_blk, pos_blk, doc_blk)
        prob_full = jnp.where(visible, jnp.exp(raw_scores - log_total[..., None]), 0.0)
        prob_low = prob_full.astype(jnp.bfloat16)
        key_heads = key_blk.reshape(key_rows, KVH, HDIM)
        value_heads = value_blk.reshape(key_rows, KVH, HDIM)
        grad_value_blk = jnp.einsum(
            "kgqt,qkgd->tkd", prob_low, grad_att, preferred_element_type=jnp.float32
        )
        grad_probs = jnp.einsum(
            "qkgd,tkd->kgqt", grad_att, value_heads, preferred_element_type=jnp.float32
        )
        grad_scores = (prob_full * (grad_probs - row_delta[..., None])).astype(jnp.bfloat16)
        grad_query = (
            grad_query
            + jnp.einsum(
                "kgqt,tkd->qkgd", grad_scores, key_heads, preferred_element_type=jnp.float32
            )
            * score_scale
        )
        grad_key_blk = (
            jnp.einsum("kgqt,qkgd->tkd", grad_scores, query_rot, preferred_element_type=jnp.float32)
            * score_scale
        )
        return (
            grad_query,
            (
                grad_key_blk.reshape(key_rows, key_width),
                grad_value_blk.reshape(key_rows, key_width),
            ),
        )

    back_keys = key_back.reshape(key_steps, key_rows, key_width)
    back_values = value_back.reshape(key_steps, key_rows, key_width)
    grad_query, (grad_key_steps, grad_value_steps) = lax.scan(
        backward_step, start_acc, (back_keys, back_values, pos_blocks, doc_blocks)
    )
    grad_key_all = grad_key_steps.reshape(seq_len, key_width)
    grad_value_all = grad_value_steps.reshape(seq_len, key_width)
    grad_key_own, grad_value_own = (
        lax.psum_scatter(
            grad_key_all.astype(jnp.bfloat16), "ctx", scatter_dimension=0, tiled=True
        ).astype(jnp.float32),
        lax.psum_scatter(
            grad_value_all.astype(jnp.bfloat16), "ctx", scatter_dimension=0, tiled=True
        ).astype(jnp.float32),
    )
    grad_query = (
        rotary(grad_query.reshape(row_count, H, HDIM), rot_cos, -rot_sin)
        .astype(jnp.bfloat16)
        .reshape(row_count, H * HDIM)
    )
    grad_key = (
        rotary(grad_key_own.reshape(row_count, KVH, HDIM), rot_cos, -rot_sin)
        .astype(jnp.bfloat16)
        .reshape(row_count, key_width)
    )
    grad_value = grad_value_own.astype(jnp.bfloat16)
    grad_w_query = contract_rows(normed, grad_query)
    grad_w_key = contract_rows(normed, grad_key)
    grad_w_value = contract_rows(normed, grad_value)
    grad_normed = (
        contract_cols(grad_query, query_w)
        + contract_cols(grad_key, key_w)
        + contract_cols(grad_value, value_w)
    )
    grad_gain_one = jnp.sum(grad_normed * inputs * scale_one, axis=0)
    grad_tokens = grad_hidden + rms_backward(inputs, scale_one, gain_one, grad_normed)
    grad_w_down = contract_rows(middle, grad_out)
    shard_gain_one, shard_out, shard_down = reduce_grads(grad_gain_one, grad_w_out, grad_w_down)
    shard_query, shard_key, shard_value = reduce_grads(grad_w_query, grad_w_key, grad_w_value)
    return (
        output,
        grad_tokens[None],
        shard_gain_one,
        shard_query,
        shard_key,
        shard_value,
        shard_out,
        shard_gain_two,
        shard_gate,
        shard_up,
        shard_down,
    )


def solution(mesh):
    placed = (
        P("seq", "ctx", None),
        P("seq", "ctx", None),
        P(("seq", "ctx")),
        P(("seq", "ctx"), None),
        P(("seq", "ctx"), None),
        P(("seq", "ctx"), None),
        P(("seq", "ctx"), None),
        P(("seq", "ctx")),
        P(("seq", "ctx"), None),
        P(("seq", "ctx"), None),
        P(("seq", "ctx"), None),
        P("seq", None),
        P("seq", None),
    )
    return jax.shard_map(
        per_device,
        mesh=mesh,
        in_specs=placed,
        out_specs=(
            P("seq", "ctx", None),
            P("seq", "ctx", None),
            P(("seq", "ctx")),
            P(("seq", "ctx"), None),
            P(("seq", "ctx"), None),
            P(("seq", "ctx"), None),
            P(("seq", "ctx"), None),
            P(("seq", "ctx")),
            P(("seq", "ctx"), None),
            P(("seq", "ctx"), None),
            P(("seq", "ctx"), None),
        ),
        check_vma=False,
    )
```

profile of v0, /device:TPU:0, one launch (start us, length us, event | category | flops | bytes accessed | tf_op | source)
XLA Modules:
  0.0 3734.7 jit_solution(5624613284984751308)
XLA Ops:
  10.5 42.6 %all-reduce.4 = (bf16[2048]{0:T(1024)(128)(2,1)S(1)}, bf16[2048]{0:T(1024)(128)(2,1)S(1)}) all-reduce(bf16[2048]{0:T(1024)(128)(2,1)S(1)} %dynamic-update-slice, bf16[2048]{0:T(1024)(128)(2,1)S(1)} %dynamic-update-slice.1), channel_id=1, replica_groups=mesh['seq'=4,'ctx'=8] {'seq','ctx'}, use_global_device_ids=true, to_apply=%add | all-reduce | flops 4096 | bytes 16384
  54.8 21.0 all-gather.10.cloned.1.call-done
  75.9 3.8 convolution_convert_fusion.8
  81.0 58.6 %all-gather.14.cloned.1.call-done = bf16[2048,1024]{1,0:T(8,128)(2,1)} async-done(((bf16[64,1024]{1,0:T(8,128)(2,1)}), bf16[2048,1024]{1,0:T(8,128)(2,1)}) %all-gather.14.cloned.1.call-update) | async-done | bytes 4194320 | tf_op jit(solution)/shard_map/all_gather | solution.py:72
  139.5 6.5 copy.96
  146.1 3.8 fusion.52
  154.4 4.5 gather_fusion
  159.1 31.0 all-gather.12.cloned.1.call-done
  190.1 3.9 copy.103
  194.1 48.1 %all-gather.16.cloned.1.call-done = bf16[1024,1024]{0,1:T(8,128)(2,1)} async-done(((bf16[128,1024]{0,1:T(8,128)(2,1)}), bf16[1024,1024]{0,1:T(8,128)(2,1)}) %all-gather.16.cloned.1.call-update) | async-done | bytes 2097168 | tf_op jit(solution)/shard_map/all_gather | solution.py:171
  242.2 3.1 copy.173
  245.3 75.4 %all-gather.18.cloned.1.call-done = bf16[2048,2048]{1,0:T(8,128)(2,1)} async-done(((bf16[64,2048]{1,0:T(8,128)(2,1)}), bf16[2048,2048]{1,0:T(8,128)(2,1)}) %all-gather.18.cloned.1.call-update) | async-done | bytes 8388624 | tf_op jit(solution)/shard_map/all_gather | solution.py:71
  320.7 12.3 copy.98
  333.0 6.3 fusion.50
  340.9 7.5 while.41
  348.4 14.9 while.42
  358.8 2.8 fusion.153
  364.6 34.9 all-gather.20.cloned.1.call-done
  399.5 4.8 multiply_reduce_fusion.3
  404.5 191.4 %all-gather.22.cloned.1.call-done = bf16[2048,8192]{1,0:T(8,128)(2,1)} async-done(((bf16[64,8192]{1,0:T(8,128)(2,1)}), bf16[2048,8192]{1,0:T(8,128)(2,1)}) %all-gather.22.cloned.1.call-update) | async-done | bytes 33554448 | tf_op jit(solution)/shard_map/all_gather | solution.py:80
  595.9 17.8 fusion.64
  613.8 178.2 %all-gather.24.cloned.1.call-done = bf16[2048,8192]{1,0:T(8,128)(2,1)} async-done(((bf16[64,8192]{1,0:T(8,128)(2,1)}), bf16[2048,8192]{1,0:T(8,128)(2,1)}) %all-gather.24.cloned.1.call-update) | async-done | bytes 33554448 | tf_op jit(solution)/shard_map/all_gather | solution.py:81
  791.9 20.7 fusion.17
  812.7 175.3 %all-gather.26.cloned.1.call-done = bf16[8192,2048]{1,0:T(8,128)(2,1)} async-done(((bf16[256,2048]{1,0:T(8,128)(2,1)}), bf16[8192,2048]{1,0:T(8,128)(2,1)}) %all-gather.26.cloned.1.call-update) | async-done | bytes 33554448 | tf_op jit(solution)/shard_map/all_gather | solution.py:82
  987.9 19.7 multiply_convert_fusion
  1007.6 17.6 fusion.65
  1025.3 16.9 multiply_reduce_fusion
  1043.6 6.4 convolution_convert_fusion.7
  1052.3 33.2 while.43
  1056.6 2.7 fusion.167
  1073.0 3.0 fusion.167
  1087.6 6.3 fusion.66
  1093.9 57.7 %reduce-scatter.23.cloned.1.call-done = bf16[128,1024]{1,0:T(8,128)(2,1)} async-done(((bf16[1024,1024]{1,0:T(8,128)(2,1)}), bf16[128,1024]{1,0:T(8,128)(2,1)}) %reduce-scatter.23.cloned.1.call-update) | async-done | bytes 262160 | tf_op jit(solution)/shard_map/reduce_scatter | solution.py:309
  1153.3 4.7 convolution_add_fusion.1
  1158.0 64.0 %reduce-scatter.25.cloned.1.call-done = bf16[128,1024]{1,0:T(8,128)(2,1)} async-done(((bf16[1024,1024]{1,0:T(8,128)(2,1)}), bf16[128,1024]{1,0:T(8,128)(2,1)}) %reduce-scatter.25.cloned.1.call-update) | async-done | bytes 262160 | tf_op jit(solution)/shard_map/reduce_scatter | solution.py:312
  1222.0 4.3 fusion.38
  1228.3 3.2 convolution_convert_fusion.6
  1231.9 3.3 convolution_convert_fusion.5
  1235.2 5.6 convolution_convert_fusion.3
  1240.9 5.6 convolution_convert_fusion.4
  1248.2 13.9 convolution_convert_fusion.1
  1263.7 13.8 convolution_convert_fusion
  1277.8 3.2 copy.143
  1281.1 14.3 convolution_convert_fusion.2
  1297.3 22.0 reduce-scatter.31.cloned.1.call-done
  1319.3 92.1 %reduce-scatter.35.cloned.1.call-done = bf16[4,64,1024]{2,1,0:T(8,128)(2,1)} async-done(((bf16[4,512,1024]{2,1,0:T(8,128)(2,1)}), bf16[4,64,1024]{2,1,0:T(8,128)(2,1)}) %reduce-scatter.35.cloned.1.call-update) | async-done | bytes 524304 | tf_op jit(solution)/shard_map/reduce_scatter | solution.py:100
  1411.5 152.6 %reduce-scatter.39.cloned.1.call-done = bf16[4,64,2048]{2,1,0:T(8,128)(2,1)} async-done(((bf16[4,512,2048]{2,1,0:T(8,128)(2,1)}), bf16[4,64,2048]{2,1,0:T(8,128)(2,1)}) %reduce-scatter.39.cloned.1.call-update) | async-done | bytes 1048592 | tf_op jit(solution)/shard_map/reduce_scatter | solution.py:97
  1564.1 152.3 %reduce-scatter.27.cloned.1.call-done = bf16[4,64,2048]{2,1,0:T(8,128)(2,1)} async-done(((bf16[4,512,2048]{2,1,0:T(8,128)(2,1)}), bf16[4,64,2048]{2,1,0:T(8,128)(2,1)}) %reduce-scatter.27.cloned.1.call-update) | async-done | bytes 1048592 | tf_op jit(solution)/shard_map/reduce_scatter | solution.py:94
  1716.5 545.7 %reduce-scatter.43.cloned.1.call-done = bf16[4,64,8192]{2,1,0:T(8,128)(2,1)} async-done(((bf16[4,512,8192]{2,1,0:T(8,128)(2,1)}), bf16[4,64,8192]{2,1,0:T(8,128)(2,1)}) %reduce-scatter.43.cloned.1.call-update) | async-done | bytes 4194320 | tf_op jit(solution)/shard_map/reduce_scatter | solution.py:97
  2262.2 545.6 %reduce-scatter.47.cloned.1.call-done = bf16[4,64,8192]{2,1,0:T(8,128)(2,1)} async-done(((bf16[4,512,8192]{2,1,0:T(8,128)(2,1)}), bf16[4,64,8192]{2,1,0:T(8,128)(2,1)}) %reduce-scatter.47.cloned.1.call-update) | async-done | bytes 4194320 | tf_op jit(solution)/shard_map/reduce_scatter | solution.py:100
  2807.9 545.6 %reduce-scatter.51.cloned.1.call-done = bf16[4,256,2048]{2,1,0:T(8,128)(2,1)} async-done(((bf16[4,2048,2048]{2,1,0:T(8,128)(2,1)}), bf16[4,256,2048]{2,1,0:T(8,128)(2,1)}) %reduce-scatter.51.cloned.1.call-update) | async-done | bytes 4194320 | tf_op jit(solution)/shard_map/reduce_scatter | solution.py:100
  3354.1 18.7 fusion.23
  3372.9 44.5 %reduce-scatter.57.cloned.1.call-done = bf16[64,4]{1,0:T(8,128)(2,1)} async-done(((bf16[512,4]{1,0:T(8,128)(2,1)}), bf16[64,4]{1,0:T(8,128)(2,1)}) %reduce-scatter.57.cloned.1.call-update) | async-done | bytes 528
  3418.2 62.9 %reduce-scatter.55.cloned.1.call-done = bf16[64,4]{1,0:T(8,128)(2,1)} async-done(((bf16[512,4]{1,0:T(8,128)(2,1)}), bf16[64,4]{1,0:T(8,128)(2,1)}) %reduce-scatter.55.cloned.1.call-update) | async-done | bytes 528
  3481.8 5.6 all-reduce.5
  3489.8 14.5 reduce-scatter.33.cloned.1.call-done
  3505.9 22.7 reduce-scatter.37.cloned.1.call-done
  3530.2 25.8 reduce-scatter.41.cloned.1.call-done
  3557.8 25.7 reduce-scatter.29.cloned.1.call-done
  3585.3 45.3 %reduce-scatter.45.cloned.1.call-done = bf16[1,64,8192]{2,1,0:T(8,128)(2,1)} async-done(((bf16[4,64,8192]{2,1,0:T(8,128)(2,1)}), bf16[1,64,8192]{2,1,0:T(8,128)(2,1)}) %reduce-scatter.45.cloned.1.call-update) | async-done | bytes 1048592 | tf_op jit(solution)/shard_map/reduce_scatter | solution.py:108
  3630.6 2.7 bitcast_convert_fusion.2
  3633.3 44.4 %reduce-scatter.49.cloned.1.call-done = bf16[1,64,8192]{2,1,0:T(8,128)(2,1)} async-done(((bf16[4,64,8192]{2,1,0:T(8,128)(2,1)}), bf16[1,64,8192]{2,1,0:T(8,128)(2,1)}) %reduce-scatter.49.cloned.1.call-update) | async-done | bytes 1048592 | tf_op jit(solution)/shard_map/reduce_scatter | solution.py:111
  3680.4 44.2 %reduce-scatter.53.cloned.1.call-done = bf16[1,256,2048]{2,1,0:T(8,128)(2,1)} async-done(((bf16[4,256,2048]{2,1,0:T(8,128)(2,1)}), bf16[1,256,2048]{2,1,0:T(8,128)(2,1)}) %reduce-scatter.53.cloned.1.call-update) | async-done | bytes 1048592 | tf_op jit(solution)/shard_map/reduce_scatter | solution.py:111
  3724.6 2.8 bitcast_convert_fusion
  (263 shorter events, 89.5 us)
Async XLA Ops:
  7.2 147.2 %copy-start = (s32[1,1024]{1,0:T(1,128)S(1)}, s32[1,1024]{1,0:T(1,128)}, u32[]{:S(2)}) copy-start(s32[1,1024]{1,0:T(1,128)} %param.31) | copy-start | bytes 12292
  7.2 72.6 %copy-start.36 = (s32[1,8]{1,0:T(1,128)S(1)}, s32[1,8]{1,0:T(1,128)}, u32[]{:S(2)}) copy-start(s32[1,8]{1,0:T(1,128)} %param.30) | copy-start | bytes 100
  7.2 68.7 %all-gather.10.cloned.1.call-start = ((), (), s32[]{:S(2)}) async-start(), calls=%async_computation.18 | async-start | bytes 4325376 | tf_op jit(solution)/shard_map/all_gather | solution.py:73
  7.9 131.6 %all-gather.14.cloned.1.call-start = ((), (), s32[]{:S(2)}) async-start(), calls=%async_computation.20 | async-start | bytes 4325376 | tf_op jit(solution)/shard_map/all_gather | solution.py:72
  8.7 181.4 %all-gather.12.cloned.1.call-start = ((), (), s32[]{:S(2)}) async-start(), calls=%async_computation.19 | async-start | bytes 2359296 | tf_op jit(solution)/shard_map/all_gather | solution.py:172
  53.1 279.9 %copy-start.31 = (f32[2048]{0:T(1024)}, f32[2048]{0:T(1024)S(1)}, u32[]{:S(2)}) copy-start(f32[2048]{0:T(1024)S(1)} %convert_element_type.201) | copy-start | bytes 24580
  54.8 278.1 %copy-start.33 = (f32[128]{0:T(128)}, f32[128]{0:T(128)S(1)}, u32[]{:S(2)}) copy-start(f32[128]{0:T(128)S(1)} %get-tuple-element.517) | copy-start | bytes 1540
  79.7 162.5 %all-gather.16.cloned.1.call-start = ((), (), s32[]{:S(2)}) async-start(), calls=%async_computation.21 | async-start | bytes 2359296 | tf_op jit(solution)/shard_map/all_gather | solution.py:171
  81.0 258.3 %copy-start.27 = (f32[128,128]{1,0:T(8,128)}, f32[128,128]{1,0:T(8,128)S(1)}, u32[]{:S(2)}) copy-start(f32[128,128]{1,0:T(8,128)S(1)} %get-tuple-element.515) | copy-start | bytes 196612
  139.5 6.6 copy-start.12
  150.9 169.8 %all-gather.18.cloned.1.call-start = ((), (), s32[]{:S(2)}) async-start(), calls=%async_computation.22 | async-start | bytes 8650752 | tf_op jit(solution)/shard_map/all_gather | solution.py:71
  151.5 248.1 %all-gather.20.cloned.1.call-start = ((), (), s32[]{:S(2)}) async-start(), calls=%async_computation.23 | async-start | bytes 8650752 | tf_op jit(solution)/shard_map/all_gather | solution.py:74
  152.0 443.9 %all-gather.22.cloned.1.call-start = ((), (), s32[]{:S(2)}) async-start(), calls=%async_computation.24 | async-start | bytes 34603008 | tf_op jit(solution)/shard_map/all_gather | solution.py:80
  152.8 639.2 %all-gather.24.cloned.1.call-start = ((), (), s32[]{:S(2)}) async-start(), calls=%async_computation.25 | async-start | bytes 34603008 | tf_op jit(solution)/shard_map/all_gather | solution.py:81
  153.5 834.4 %all-gather.26.cloned.1.call-start = ((), (), s32[]{:S(2)}) async-start(), calls=%async_computation.26 | async-start | bytes 34603008 | tf_op jit(solution)/shard_map/all_gather | solution.py:82
  154.3 997.3 %reduce-scatter.23.cloned.1.call-start = ((), (), s32[]{:S(2)}) async-start(), calls=%async_computation.27 | async-start | bytes 2359296 | tf_op jit(solution)/shard_map/reduce_scatter | solution.py:309
  352.1 1.5 copy-start.6
  358.8 2.8 copy-start.6
  364.6 39.7 %copy-start.23 = (bf16[128,4,2,256]{0,3,2,1:T(8,128)(2,1)}, bf16[128,4,2,256]{0,3,2,1:T(8,128)(2,1)S(1)}, u32[]{:S(2)}) copy-start(bf16[128,4,2,256]{0,3,2,1:T(8,128)(2,1)S(1)} %convert_element_type.209) | copy-start | bytes 1572868
  404.3 637.9 %copy-start.16 = (f32[128,2048]{1,0:T(8,128)}, f32[128,2048]{1,0:T(8,128)S(1)}, u32[]{:S(2)}) copy-start(f32[128,2048]{1,0:T(8,128)S(1)} %get-tuple-element.523) | copy-start | bytes 3145732
  404.5 387.4 %copy-start.21 = (bf16[128,2048]{1,0:T(8,128)(2,1)}, bf16[128,2048]{1,0:T(8,128)(2,1)S(1)}, u32[]{:S(2)}) copy-start(bf16[128,2048]{1,0:T(8,128)(2,1)S(1)} %multiply_convert_fusion.4) | copy-start | bytes 1572868
  1007.6 17.7 copy-start.18
  1025.3 17.0 copy-start.25
  1043.6 7.4 copy-start.4
  1043.6 7.4 copy-start.8
  1043.6 8.7 copy-start.10
  1052.5 2.4 copy-start.3
  1065.8 3.1 copy-start.11
  1068.8 2.4 copy-start.3
  1082.4 3.1 copy-start.11
  1085.5 1.2 copy-start.5
  1085.5 1.6 copy-start.28
  1085.5 1.6 copy-start.30
  1085.5 136.5 %reduce-scatter.25.cloned.1.call-start = ((), (), s32[]{:S(2)}) async-start(), calls=%async_computation.28 | async-start | bytes 2359296 | tf_op jit(solution)/shard_map/reduce_scatter | solution.py:312
  1086.3 233.0 %reduce-scatter.31.cloned.1.call-start = ((), (), s32[]{:S(2)}) async-start(), calls=%async_computation.31 | async-start | bytes 4718592 | tf_op jit(solution)/shard_map/reduce_scatter | solution.py:97
  1153.0 69.0 %copy-start.13 = (bf16[1,128,2048]{2,1,0:T(8,128)(2,1)S(1)}, bf16[1,128,2048]{2,1,0:T(8,128)(2,1)}, u32[]{:S(2)}) copy-start(bf16[1,128,2048]{2,1,0:T(8,128)(2,1)} %param.19) | copy-start | bytes 1572868
  1153.0 69.0 %copy-start.32 = (f32[2048]{0:T(1024)S(1)}, f32[2048]{0:T(1024)}, u32[]{:S(2)}) copy-start(f32[2048]{0:T(1024)} %copy-done.31) | copy-start | bytes 24580
  1153.0 69.0 %copy-start.34 = (f32[128]{0:T(128)S(1)}, f32[128]{0:T(128)}, u32[]{:S(2)}) copy-start(f32[128]{0:T(128)} %copy-done.33) | copy-start | bytes 1540
  1158.0 68.3 %copy-start.15 = (f32[128,2048]{1,0:T(8,128)S(1)}, f32[128,2048]{1,0:T(8,128)}, u32[]{:S(2)}) copy-start(f32[128,2048]{1,0:T(8,128)} %copy-done.14) | copy-start | bytes 3145732
  1158.0 68.3 %copy-start.35 = (f32[128]{0:T(128)S(1)}, f32[128]{0:T(128)}, u32[]{:S(2)}) copy-start(f32[128]{0:T(128)} %get-tuple-element.516) | copy-start | bytes 1540
  1228.3 3.5 copy-start.29
  1231.6 3.6 copy-start.24
  1231.6 179.8 %reduce-scatter.35.cloned.1.call-start = ((), (), s32[]{:S(2)}) async-start(), calls=%async_computation.33 | async-start | bytes 4718592 | tf_op jit(solution)/shard_map/reduce_scatter | solution.py:100
  1235.2 328.9 %reduce-scatter.39.cloned.1.call-start = ((), (), s32[]{:S(2)}) async-start(), calls=%async_computation.35 | async-start | bytes 9437184 | tf_op jit(solution)/shard_map/reduce_scatter | solution.py:97
  1240.9 475.5 %reduce-scatter.27.cloned.1.call-start = ((), (), s32[]{:S(2)}) async-start(), calls=%async_computation.29 | async-start | bytes 9437184 | tf_op jit(solution)/shard_map/reduce_scatter | solution.py:94
  1246.6 1.6 copy-start.19
  1246.6 1.7 copy-start.22
  1246.6 1015.6 %reduce-scatter.43.cloned.1.call-start = ((), (), s32[]{:S(2)}) async-start(), calls=%async_computation.37 | async-start | bytes 37748736 | tf_op jit(solution)/shard_map/reduce_scatter | solution.py:97
  1262.1 1.6 copy-start.20
  1262.1 1545.7 %reduce-scatter.47.cloned.1.call-start = ((), (), s32[]{:S(2)}) async-start(), calls=%async_computation.39 | async-start | bytes 37748736 | tf_op jit(solution)/shard_map/reduce_scatter | solution.py:100
  1277.5 3.6 copy-start.26
  1277.5 2076.0 %reduce-scatter.51.cloned.1.call-start = ((), (), s32[]{:S(2)}) async-start(), calls=%async_computation.41 | async-start | bytes 37748736 | tf_op jit(solution)/shard_map/reduce_scatter | solution.py:100
  1295.4 2122.0 %reduce-scatter.57.cloned.1.call-start = ((), (), s32[]{:S(2)}) async-start(), calls=%async_computation.44 | async-start | bytes 147456
  1296.3 2184.7 %reduce-scatter.55.cloned.1.call-start = ((), (), s32[]{:S(2)}) async-start(), calls=%async_computation.43 | async-start | bytes 147456
  1297.2 2207.1 %reduce-scatter.33.cloned.1.call-start = ((), (), s32[]{:S(2)}) async-start(), calls=%async_computation.32 | async-start | bytes 655360 | tf_op jit(solution)/shard_map/reduce_scatter | solution.py:108
  1319.3 2209.3 %reduce-scatter.37.cloned.1.call-start = ((), (), s32[]{:S(2)}) async-start(), calls=%async_computation.34 | async-start | bytes 655360 | tf_op jit(solution)/shard_map/reduce_scatter | solution.py:111
  1411.4 2144.6 %reduce-scatter.41.cloned.1.call-start = ((), (), s32[]{:S(2)}) async-start(), calls=%async_computation.36 | async-start | bytes 1310720 | tf_op jit(solution)/shard_map/reduce_scatter | solution.py:108
  1564.1 2019.4 %reduce-scatter.29.cloned.1.call-start = ((), (), s32[]{:S(2)}) async-start(), calls=%async_computation.30 | async-start | bytes 1310720 | tf_op jit(solution)/shard_map/reduce_scatter | solution.py:105
  1716.4 1914.2 %reduce-scatter.45.cloned.1.call-start = ((), (), s32[]{:S(2)}) async-start(), calls=%async_computation.38 | async-start | bytes 5242880 | tf_op jit(solution)/shard_map/reduce_scatter | solution.py:108
  2262.2 1415.5 %reduce-scatter.49.cloned.1.call-start = ((), (), s32[]{:S(2)}) async-start(), calls=%async_computation.40 | async-start | bytes 5242880 | tf_op jit(solution)/shard_map/reduce_scatter | solution.py:111
  2807.9 545.7 %copy-start.37 = (u32[32]{0:T(128)S(1)}, u32[32]{0:T(128)}, u32[]{:S(2)}) copy-start(u32[32]{0:T(128)} %constant.115) | copy-start | bytes 388
  2807.9 546.3 %copy-start.17 = (f32[128,2048]{1,0:T(8,128)S(1)}, f32[128,2048]{1,0:T(8,128)}, u32[]{:S(2)}) copy-start(f32[128,2048]{1,0:T(8,128)} %copy-done.16) | copy-start | bytes 3145732
  2807.9 916.7 %reduce-scatter.53.cloned.1.call-start = ((), (), s32[]{:S(2)}) async-start(), calls=%async_computation.42 | async-start | bytes 5242880 | tf_op jit(solution)/shard_map/reduce_scatter | solution.py:111
  3583.5 143.9 %copy-start.1 = (s32[1,1024]{1,0:T(1,128)S(1)}, s32[1,1024]{1,0:T(1,128)}, u32[]{:S(2)}) copy-start(s32[1,1024]{1,0:T(1,128)} %param.31) | copy-start | bytes 12292
  (6 other events, 6.1 us)
Sparse Core Ops, SparseCore 0:
  11.0 64.7 all-gather.9
  78.9 60.6 all-gather.13
  142.2 47.8 all-gather.11
  192.6 49.5 all-gather.15
  245.0 75.5 all-gather.17
  323.5 75.9 all-gather.19
  402.5 193.3 all-gather.21
  598.9 192.9 all-gather.23
  794.9 192.9 all-gather.25
  1085.6 65.9 reduce-scatter.22
  1155.1 66.8 reduce-scatter.24
  1231.7 87.4 reduce-scatter.30
  1323.3 88.0 reduce-scatter.34
  1414.9 149.0 reduce-scatter.38
  1568.0 148.3 reduce-scatter.26
  1720.0 542.0 reduce-scatter.42
  2265.8 542.0 reduce-scatter.46
  2811.5 541.9 reduce-scatter.50
  3357.4 59.9 reduce-scatter.56
  3421.1 59.8 reduce-scatter.54
  3483.5 20.6 reduce-scatter.32
  3506.9 21.6 reduce-scatter.36
  3531.1 24.8 reduce-scatter.40
  3558.6 24.8 reduce-scatter.28
  3586.0 44.4 reduce-scatter.44
  3633.1 44.5 reduce-scatter.48
  3680.0 44.4 reduce-scatter.52
where the time goes:
time: 3750 us; the launch traced here: 3730 us
  waiting for transfers between devices  3330 us (89%)
  matrix products  244 us (7%)
  local copies, waits for them, and re-layouts  69.7 us (2%)
  blocking collectives  48.3 us (1%)
    reduce_scatter x3, waiting for transfers between devices, reduce_grads(): lax.psum_scatter(grad_three.astype(jnp.bfloat16), 'ctx', scatter_dimensio...  1180 us
    reduce_scatter x3, waiting for transfers between devices, reduce_grads(): lax.psum_scatter(grad_two.astype(jnp.bfloat16), 'ctx', scatter_dimension=...  720 us
    all_gather x1, waiting for transfers between devices, mlp_weights(): lax.all_gather(w_gate, ('seq', 'ctx'), axis=0, tiled=True)  191 us
    all_gather x1, waiting for transfers between devices, mlp_weights(): lax.all_gather(w_up, ('seq', 'ctx'), axis=0, tiled=True)  178 us
    all_gather x1, waiting for transfers between devices, mlp_weights(): lax.all_gather(w_down, ('seq', 'ctx'), axis=0, tiled=True)  175 us
    reduce_scatter x1, waiting for transfers between devices, reduce_grads(): lax.psum_scatter(grad_one.astype(jnp.bfloat16), 'ctx', scatter_dimension=...  152 us
    unnamed x29, waiting for transfers between devices  113 us
    reduce_scatter x3, waiting for transfers between devices, reduce_grads(): lax.psum_scatter(grad_three.astype(jnp.bfloat16), 'seq', scatter_dimensio...  111 us
  transfers between devices with their start and end apart: 27, of which 27 were waited for; matrix products, arithmetic and copies ran while one was open for 6% of the time, Pallas kernels for 0%

commit v1 on v0

--- a/solution.py
+++ b/solution.py
@@ -1,8 +1,11 @@
+import functools
 import math
 
 import jax
 import jax.numpy as jnp
 from jax import lax
+from jax.experimental import pallas as pl
+from jax.experimental.pallas import tpu as pltpu
 from jax.sharding import PartitionSpec as P
 
 H = 8
@@ -115,7 +118,7 @@
     return (grad_one[0], grad_two[0], grad_three[0])
 
 
-def per_device(
+def general_device(
     tokens,
     cotangent,
     gain_attn,
@@ -352,6 +355,579 @@
     )
 
 
+MESH = pl.DeviceIdType.MESH
+VMEM = pltpu.VMEM
+RING = 8
+SEQ = 4
+
+
+class Place:
+    def __init__(self):
+        self.c = lax.axis_index("ctx")
+        self.s = lax.axis_index("seq")
+        z, x = self.c // 2, lax.rem(self.c, 2)
+        self.p = z + x * (7 - 2 * z)
+        self.right = {"ctx": self.at(1)}
+        self.left = {"ctx": self.at(-1)}
+        self.s_core = self.s + 1 - 2 * lax.rem(self.s, 2)
+        self.s_far = lax.rem(self.s + 2, 4)
+        self.s_both = 3 - self.s
+        self.core_peer = {"seq": self.s_core}
+        self.far_peer = {"seq": self.s_far}
+
+    def at(self, offset):
+        q = lax.rem(self.p + offset + 2 * RING, RING)
+        return 2 * q + (q // 4) * (15 - 4 * q)
+
+    def peers(self):
+        return [{"ctx": lax.rem(self.c + k, RING)} for k in range(1, RING)]
+
+
+def greet(devices):
+    barrier = pltpu.get_barrier_semaphore()
+    for device in devices:
+        pl.semaphore_signal(barrier, inc=1, device_id=device, device_id_type=MESH)
+    pl.semaphore_wait(barrier, len(devices))
+
+
+def remote(src, dst, send_sem, recv_sem, device):
+    return pltpu.make_async_remote_copy(
+        src_ref=src, dst_ref=dst, send_sem=send_sem, recv_sem=recv_sem, device_id=device, device_id_type=MESH
+    )
+
+
+def arrived(ref, sems, index, device):
+    remote(ref, ref, sems[0].at[index], sems[1].at[index], device).wait_recv()
+
+
+def together(*flows):
+    live = list(flows)
+    while live:
+        live = [flow for flow in live if next(flow, "end") != "end"]
+
+
+def ring_sems():
+    return [pltpu.SemaphoreType.DMA((2, RING // 2, 2))] * 2
+
+
+def ring_gather(own, buf, sems, place):
+    half = own.shape[0] // 2
+    steps = RING // 2
+    sent = []
+
+    def part(ref, j):
+        return ref.at[pl.ds(j * half, half)]
+
+    def owner(d, s):
+        return place.at(-s if d == 0 else s)
+
+    def wait_for(d, s, j):
+        arrived(part(buf.at[owner(d, s + 1)], j), sems, (d, s, j), place.right if d == 0 else place.left)
+
+    for s in range(steps):
+        for j in range(2):
+            for d in range(2):
+                if s == steps - 1 and j != d:
+                    continue
+                if s > 0:
+                    wait_for(d, s - 1, j)
+                copy = remote(
+                    part(own if s == 0 else buf.at[owner(d, s)], j),
+                    part(buf.at[owner(d, s)], j),
+                    sems[0].at[d, s, j],
+                    sems[1].at[d, s, j],
+                    place.right if d == 0 else place.left,
+                )
+                copy.start()
+                sent.append(copy)
+            yield
+    for d in range(2):
+        wait_for(d, steps - 2, 1 - d)
+        wait_for(d, steps - 1, d)
+        yield
+    for copy in sent:
+        copy.wait_send()
+
+
+def ring_scatter(part, out, slots, sems, place):
+    half = part.shape[1] // 2
+    steps = RING // 2
+    sent = []
+
+    def rows(ref, j):
+        return ref.at[pl.ds(j * half, half)]
+
+    def block(d, s):
+        return place.at(steps - s if d == 0 else s - steps)
+
+    def side(d):
+        return place.right if d == 0 else place.left
+
+    for s in range(steps):
+        for j in range(2):
+            for d in range(2):
+                if s == 0 and j != d:
+                    continue
+                source = rows(part.at[block(d, s)], j)
+                if s > 1 or (s == 1 and j == d):
+                    held = rows(slots.at[d, s - 1], j)
+                    arrived(held, sems, (d, s - 1, j), side(d))
+                    held[...] = (held[...].astype(jnp.float32) + source[...].astype(jnp.float32)).astype(held.dtype)
+                    source = held
+                copy = remote(source, rows(slots.at[d, s], j), sems[0].at[d, s, j], sems[1].at[d, s, j], side(d))
+                copy.start()
+                sent.append(copy)
+            yield
+    for j in range(2):
+        total = rows(part.at[place.c], j)[...].astype(jnp.float32)
+        for d in range(2):
+            held = rows(slots.at[d, steps - 1], j)
+            arrived(held, sems, (d, steps - 1, j), side(d))
+            total = total + held[...].astype(jnp.float32)
+        rows(out, j)[...] = total
+        yield
+    for copy in sent:
+        copy.wait_send()
+
+
+def pair_sems():
+    return [pltpu.SemaphoreType.DMA((RING,))] * 2
+
+
+def exchange(src, buf, sems, place):
+    sent = []
+    for k in range(1, RING):
+        to = lax.rem(place.c + k, RING)
+        copy = remote(src.at[to], buf.at[place.c], sems[0].at[k], sems[1].at[k], {"ctx": to})
+        copy.start()
+        sent.append(copy)
+    yield
+    for k in range(1, RING):
+        source = lax.rem(place.c + RING - k, RING)
+        arrived(buf.at[source], sems, k, {"ctx": source})
+    for copy in sent:
+        copy.wait_send()
+    yield
+
+
+def seq_sems():
+    return [pltpu.SemaphoreType.DMA((3,))] * 2
+
+
+def seq_gather(own, buf, sems, place):
+    first = remote(own, buf.at[place.s], sems[0].at[0], sems[1].at[0], place.far_peer)
+    second = remote(own, buf.at[place.s], sems[0].at[1], sems[1].at[1], place.core_peer)
+    first.start()
+    second.start()
+    yield
+    arrived(buf.at[place.s_far], sems, 0, place.far_peer)
+    third = remote(buf.at[place.s_far], buf.at[place.s_far], sems[0].at[2], sems[1].at[2], place.core_peer)
+    third.start()
+    yield
+    arrived(buf.at[place.s_core], sems, 1, place.core_peer)
+    arrived(buf.at[place.s_both], sems, 2, place.core_peer)
+    for copy in (first, second, third):
+        copy.wait_send()
+    yield
+
+
+def add_into(dst, other):
+    rows = dst.shape[0]
+    step = math.gcd(rows, 32)
+
+    @pl.loop(0, rows // step)
+    def _(i):
+        at = pl.ds(pl.multiple_of(i * step, step), step)
+        dst[at] = (dst[at].astype(jnp.float32) + other[at].astype(jnp.float32)).astype(dst.dtype)
+
+
+def seq_scatter(part, near, far, sems, place):
+    low = lax.rem(place.s, 2)
+    row = place.s // 2
+    other_row = 1 - row
+    sent = []
+    for k, r in enumerate((other_row, row)):
+        copy = remote(part.at[r * 2 + 1 - low], near.at[k], sems[0].at[k], sems[1].at[k], place.core_peer)
+        copy.start()
+        sent.append(copy)
+    yield
+    arrived(near.at[0], sems, 0, place.core_peer)
+    add_into(near.at[0], part.at[other_row * 2 + low])
+    copy = remote(near.at[0], far.at[0], sems[0].at[2], sems[1].at[2], place.far_peer)
+    copy.start()
+    sent.append(copy)
+    yield
+    arrived(near.at[1], sems, 1, place.core_peer)
+    add_into(near.at[1], part.at[row * 2 + low])
+    yield
+    arrived(far.at[0], sems, 2, place.far_peer)
+    add_into(far.at[0], near.at[1])
+    for copy in sent:
+        copy.wait_send()
+    yield
+
+
+def call(body, outs, args, spaces, out_spaces, scratch, ident):
+    return pl.pallas_call(
+        body,
+        out_shape=outs,
+        in_specs=[pl.BlockSpec(memory_space=space) for space in spaces],
+        out_specs=[pl.BlockSpec(memory_space=space) for space in out_spaces],
+        scratch_shapes=scratch,
+        compiler_params=pltpu.CompilerParams(
+            collective_id=ident, has_side_effects=True, vmem_limit_bytes=56 * 1024 * 1024
+        ),
+    )(*args)
+
+
+def shaped(shape, dtype=jnp.bfloat16):
+    return jax.ShapeDtypeStruct(shape, dtype)
+
+
+def start_kernel(x, wqkv, wout, x_all, wqkv_all, wout_all, local, r0, r1, e0, e1, q0, q1, o0, o1, w0, w1):
+    place = Place()
+    greet(place.peers() + [place.core_peer, place.far_peer])
+    keep = [
+        pltpu.make_async_copy(x, x_all.at[place.c], local.at[0]),
+        pltpu.make_async_copy(wqkv.at[place.c], wqkv_all.at[place.s, place.c], local.at[1]),
+        pltpu.make_async_copy(wout, wout_all.at[place.s, place.c], local.at[2]),
+    ]
+    for copy in keep:
+        copy.start()
+
+    def attention_weights_flow():
+        yield from exchange(wqkv, wqkv_all.at[place.s], (e0, e1), place)
+        keep[1].wait()
+        yield from seq_gather(wqkv_all.at[place.s], wqkv_all, (q0, q1), place)
+
+    together(attention_weights_flow(), ring_gather(x, x_all, (r0, r1), place))
+
+    def out_weights_flow():
+        yield from ring_gather(wout, wout_all.at[place.s], (o0, o1), place)
+        keep[2].wait()
+        yield from seq_gather(wout_all.at[place.s], wout_all, (w0, w1), place)
+
+    together(out_weights_flow())
+    keep[0].wait()
+
+
+def middle_kernel(ob, dy, wcol, wdown, ob_all, dy_all, wcol_all, wdown_all, local, a0, a1, r0, r1, e0, e1, q0, q1, w0, w1):
+    place = Place()
+    greet(place.peers() + [place.core_peer, place.far_peer])
+    keep = [
+        pltpu.make_async_copy(ob.at[place.c], ob_all.at[place.c], local.at[0]),
+        pltpu.make_async_copy(dy, dy_all.at[place.c], local.at[1]),
+        pltpu.make_async_copy(wcol.at[place.c], wcol_all.at[place.s, place.c], local.at[2]),
+        pltpu.make_async_copy(wdown, wdown_all.at[place.s], local.at[3]),
+    ]
+    for copy in keep:
+        copy.start()
+
+    def columns_flow():
+        yield from exchange(wcol, wcol_all.at[place.s], (e0, e1), place)
+        keep[2].wait()
+        yield from seq_gather(wcol_all.at[place.s], wcol_all, (q0, q1), place)
+
+    together(
+        exchange(ob, ob_all, (a0, a1), place),
+        columns_flow(),
+        seq_gather(wdown, wdown_all, (w0, w1), place),
+        ring_gather(dy, dy_all, (r0, r1), place),
+    )
+    keep[0].wait()
+    keep[1].wait()
+    keep[3].wait()
+
+
+def gather_kernel(x, x_all, local, r0, r1):
+    place = Place()
+    greet([place.right, place.left])
+    keep = pltpu.make_async_copy(x, x_all.at[place.c], local)
+    keep.start()
+    together(ring_gather(x, x_all, (r0, r1), place))
+    keep.wait()
+
+
+def scatter_kernel(count, *refs):
+    parts, outs, slots, sems = refs[:count], refs[count : 2 * count], refs[2 * count : 3 * count], refs[3 * count :]
+    place = Place()
+    greet([place.right, place.left])
+    for i in range(count):
+        together(ring_scatter(parts[i], outs[i], slots[i], sems[2 * i : 2 * i + 2], place))
+
+
+def swap_kernel(x, x_all, local, a0, a1):
+    place = Place()
+    greet(place.peers())
+    keep = pltpu.make_async_copy(x.at[place.c], x_all.at[place.c], local)
+    keep.start()
+    together(exchange(x, x_all, (a0, a1), place))
+    keep.wait()
+
+
+def grads_kernel(col, down, qkv, out, col_out, down_out, qkv_out, out_out,
+                 cn, cf, dn, df, qn, qf, on, of, slots, local, c0, c1, d0, d1, k0, k1, u0, u1, e0, e1, f0, f1, g0, g1):
+    place = Place()
+    greet(place.peers() + [place.core_peer, place.far_peer])
+
+    def col_flow():
+        yield from seq_scatter(col, cn, cf, (c0, c1), place)
+        ref = cf.at[0]
+        keep = pltpu.make_async_copy(ref.at[pl.ds(pl.multiple_of(place.c * 64, 64), 64)], col_out.at[place.c], local.at[0])
+        keep.start()
+        yield from exchange(Blocks(ref, 64), col_out, (e0, e1), place)
+        keep.wait()
+
+    def qkv_flow():
+        yield from seq_scatter(qkv, qn, qf, (k0, k1), place)
+        ref = qf.at[0]
+        keep = pltpu.make_async_copy(ref.at[pl.ds(pl.multiple_of(place.c * 64, 64), 64)], qkv_out.at[place.c], local.at[1])
+        keep.start()
+        yield from exchange(Blocks(ref, 64), qkv_out, (f0, f1), place)
+        keep.wait()
+
+    def down_flow():
+        yield from seq_scatter(down, dn, df, (d0, d1), place)
+        keep = pltpu.make_async_copy(df.at[0], down_out, local.at[2])
+        keep.start()
+        keep.wait()
+
+    def out_flow():
+        yield from seq_scatter(out, on, of, (u0, u1), place)
+        yield from ring_scatter(Blocks(of.at[0], 64), out_out, slots, (g0, g1), place)
+
+    together(out_flow(), col_flow(), qkv_flow(), down_flow())
+
+
+class Blocks:
+    def __init__(self, ref, rows):
+        self.ref, self.rows = ref, rows
+        self.shape = (ref.shape[0] // rows, rows) + tuple(ref.shape[1:])
+
+    @property
+    def at(self):
+        return self
+
+    def __getitem__(self, i):
+        return self.ref.at[pl.ds(pl.multiple_of(i * self.rows, self.rows), self.rows)]
+
+
+DMA = pltpu.SemaphoreType.DMA
+HBM = pl.ANY
+
+
+def ring_device(
+    tokens, cotangent, gain_attn, w_query, w_key, w_value, w_out, gain_mlp, w_gate, w_up, w_down, pair_order, segments
+):
+    bf16, f32 = jnp.bfloat16, jnp.float32
+    n, c = RING, lax.axis_index("ctx")
+    rows, width = tokens.shape[1], tokens.shape[2]
+    half_rows, seq_len = rows // 2, segments.shape[1]
+    shard = w_query.shape[0]
+    ff_own = w_down.shape[0]
+    ff_mine = SEQ * ff_own
+    head = HDIM
+    scale = HDIM ** (-0.5)
+
+    gain_one = gain_attn.astype(f32)[:, None]
+    gain_two = gain_mlp.astype(f32)[:, None]
+    wq, wk, wv, wg, wu = (w.astype(f32) for w in (w_query, w_key, w_value, w_gate, w_up))
+    groups = H // KVH
+
+    def by_head(w):
+        return jnp.repeat((w * gain_one).astype(bf16).reshape(shard, KVH, head), groups, axis=1)
+
+    wqkv = jnp.concatenate(
+        [(wq * gain_one).astype(bf16).reshape(shard, H, head), by_head(wk), by_head(wv)], axis=-1
+    ).transpose(1, 0, 2)
+
+    def by_context(w):
+        return (w * gain_two).astype(bf16).reshape(shard, SEQ, n, ff_own).transpose(2, 0, 1, 3).reshape(n, shard, ff_mine)
+
+    wcol = jnp.concatenate([by_context(wg), by_context(wu)], axis=-1)
+
+    inputs = tokens[0].astype(f32)
+    scale_one = rms_scale(inputs)
+    xhat = (inputs * scale_one).astype(bf16)
+
+    x_all, wqkv_all, wout_all = call(
+        start_kernel,
+        [shaped((n, rows, width)), shaped((SEQ, n, shard, 3 * head)), shaped((SEQ, n, shard, width))],
+        (xhat, wqkv, w_out),
+        [HBM] * 3,
+        [HBM] * 3,
+        [DMA((3,))] + ring_sems() + pair_sems() + seq_sems() + ring_sems() + seq_sems(),
+        0,
+    )
+    x_all = x_all.reshape(seq_len, width)
+    wqkv_all = wqkv_all.reshape(width, 3 * head)
+    wout_all = wout_all.reshape(H * head, width)
+
+    block = pair_order[0]
+    blocks = jnp.stack([block, 2 * n - 1 - block], axis=1).reshape(-1)
+    pos = (blocks[:, None] * half_rows + jnp.arange(half_rows, dtype=jnp.int32)[None, :]).reshape(-1)
+    doc = jnp.take(segments[0].reshape(2 * n, half_rows), blocks, axis=0).reshape(-1)
+    angles_of = rotary_tables(pos, HDIM)
+    cos, sin = angles_of[0][:, 0], angles_of[1][:, 0]
+
+    def rot(t, sign):
+        a, b = t[:, : head // 2], t[:, head // 2 :]
+        return jnp.concatenate([a * cos - sign * b * sin, b * cos + sign * a * sin], axis=-1)
+
+    qkv = jnp.dot(x_all, wqkv_all, preferred_element_type=f32)
+    q = rot(qkv[:, :head], 1.0).astype(bf16)
+    k = rot(qkv[:, head : 2 * head], 1.0).astype(bf16)
+    v = qkv[:, 2 * head :].astype(bf16)
+    scores = contract_cols(q, k) * scale
+    visible = (doc[None, :] == doc[:, None]) & (pos[None, :] <= pos[:, None])
+    scores = jnp.where(visible, scores, NEG_FILL)
+    top = jnp.max(scores, axis=-1, keepdims=True)
+    weight = jnp.exp(scores - top)
+    prob = weight / jnp.sum(weight, axis=-1, keepdims=True)
+    prob_low = prob.astype(bf16)
+    ob = jnp.dot(prob_low, v, preferred_element_type=f32).astype(bf16)
+
+    ob_all, dy_all, wcol_all, wdown_all = call(
+        middle_kernel,
+        [
+            shaped((n, rows, head)),
+            shaped((n, rows, width)),
+            shaped((SEQ, n, shard, 2 * ff_mine)),
+            shaped((SEQ, ff_own, width)),
+        ],
+        (ob.reshape(n, rows, head), cotangent[0], wcol, w_down),
+        [HBM] * 4,
+        [HBM] * 4,
+        [DMA((4,))] + pair_sems() + ring_sems() + pair_sems() + seq_sems() + seq_sems(),
+        1,
+    )
+    ob_local = ob_all.transpose(1, 0, 2).reshape(rows, H * head)
+    dy_all = dy_all.reshape(seq_len, width)
+    wcol_all = wcol_all.reshape(width, 2 * ff_mine)
+    wdown_all = wdown_all.reshape(ff_mine, width)
+
+    hidden = inputs + jnp.dot(ob_local, wout_all, preferred_element_type=f32)
+    scale_two = rms_scale(hidden)
+    hhat = (hidden * scale_two).astype(bf16)
+    (h_all,) = call(
+        gather_kernel, [shaped((n, rows, width))], (hhat,), [HBM], [HBM], [DMA] + ring_sems(), 2
+    )
+    h_all = h_all.reshape(seq_len, width)
+    gu = jnp.dot(h_all, wcol_all, preferred_element_type=f32)
+    gate, up = gu[:, :ff_mine], gu[:, ff_mine:]
+    sig = jax.nn.sigmoid(gate)
+    active = gate * sig
+    mid = (active * up).astype(bf16)
+    dmid = contract_cols(dy_all, wdown_all)
+    dgate = (dmid * up * sig * (1.0 + gate * (1.0 - sig))).astype(bf16)
+    dup = (dmid * active).astype(bf16)
+    dgu = jnp.concatenate([dgate, dup], axis=-1)
+    part_h = contract_cols(dgu, wcol_all).astype(bf16)
+    part_out = jnp.dot(mid, wdown_all, preferred_element_type=f32).astype(bf16)
+    slot = VMEM((2, n // 2, rows, width), bf16)
+    dweighted, out_sum = call(
+        functools.partial(scatter_kernel, 2),
+        [shaped((rows, width), f32)] * 2,
+        (part_h.reshape(n, rows, width), part_out.reshape(n, rows, width)),
+        [VMEM] * 2,
+        [VMEM] * 2,
+        [slot, slot] + ring_sems() + ring_sems(),
+        3,
+    )
+    output = (hidden + out_sum).astype(bf16)[None]
+
+    def norm_back(tensor, scale_rows, weighted):
+        inner = jnp.mean(weighted * tensor, axis=-1, keepdims=True)
+        return scale_rows * weighted - tensor * (scale_rows * scale_rows * scale_rows) * inner
+
+    grad_hidden = cotangent[0].astype(f32) + norm_back(hidden, scale_two, dweighted)
+    branch = grad_hidden.astype(bf16)
+    datt = contract_cols(branch, wout_all).astype(bf16)
+    (datt_all,) = call(
+        swap_kernel,
+        [shaped((n, rows, head))],
+        (datt.reshape(rows, n, head).transpose(1, 0, 2),),
+        [HBM],
+        [HBM],
+        [DMA] + pair_sems(),
+        4,
+    )
+    datt_all = datt_all.reshape(seq_len, head)
+    dprob = contract_cols(datt_all, v)
+    delta = jnp.sum(prob * dprob, axis=-1, keepdims=True)
+    dscore = (prob * (dprob - delta)).astype(bf16)
+    dq = rot(jnp.dot(dscore, k, preferred_element_type=f32) * scale, -1.0)
+    dk = rot(contract_rows(dscore, q) * scale, -1.0)
+    dv = contract_rows(prob_low, datt_all)
+    dqkv = jnp.concatenate([dq, dk, dv], axis=-1).astype(bf16)
+    part_x = contract_cols(dqkv, wqkv_all).astype(bf16)
+    (xweighted,) = call(
+        functools.partial(scatter_kernel, 1),
+        [shaped((rows, width), f32)],
+        (part_x.reshape(n, rows, width),),
+        [VMEM],
+        [VMEM],
+        [slot] + ring_sems(),
+        5,
+    )
+    grad_tokens = grad_hidden + norm_back(inputs, scale_one, xweighted)
+
+    g_col = contract_rows(h_all, dgu).astype(bf16).reshape(SEQ, n * shard, 2 * ff_mine)
+    g_down = contract_rows(mid, dy_all).astype(bf16).reshape(SEQ, ff_own, width)
+    g_qkv = contract_rows(x_all, dqkv).astype(bf16).reshape(SEQ, n * shard, 3 * head)
+    g_out = contract_rows(ob_local, branch).astype(bf16).reshape(SEQ, n * shard, width)
+    pieces = (g_col, g_down, g_qkv, g_out)
+    near = []
+    for piece in pieces:
+        near += [VMEM((2,) + piece.shape[1:], bf16), VMEM((1,) + piece.shape[1:], bf16)]
+    col_sum, down_sum, qkv_sum, out_grad = call(
+        grads_kernel,
+        [
+            shaped((n, shard, 2 * ff_mine)),
+            shaped((ff_own, width)),
+            shaped((n, shard, 3 * head)),
+            shaped((shard, width), f32),
+        ],
+        pieces,
+        [VMEM] * 4,
+        [HBM, HBM, HBM, VMEM],
+        near
+        + [VMEM((2, n // 2, shard, width), bf16), DMA((3,))]
+        + seq_sems() * 4
+        + pair_sems() * 2
+        + ring_sems(),
+        6,
+    )
+    col_sum = col_sum.astype(f32)
+
+    def own_columns(t):
+        return t.reshape(n, shard, SEQ, ff_own).transpose(1, 2, 0, 3).reshape(shard, SEQ * n * ff_own)
+
+    raw_gate, raw_up = own_columns(col_sum[..., :ff_mine]), own_columns(col_sum[..., ff_mine:])
+    qkv_sum = qkv_sum.astype(f32)
+    raw_q = qkv_sum[..., :head].transpose(1, 0, 2).reshape(shard, H * head)
+
+    def kv_sum(t):
+        return t.reshape(KVH, groups, shard, head).sum(axis=1).transpose(1, 0, 2).reshape(shard, KVH * head)
+
+    raw_k, raw_v = kv_sum(qkv_sum[..., head : 2 * head]), kv_sum(qkv_sum[..., 2 * head :])
+    grad_gain_one = jnp.sum(raw_q * wq, axis=1) + jnp.sum(raw_k * wk, axis=1) + jnp.sum(raw_v * wv, axis=1)
+    grad_gain_two = jnp.sum(raw_gate * wg, axis=1) + jnp.sum(raw_up * wu, axis=1)
+    return (
+        output,
+        grad_tokens[None],
+        grad_gain_one,
+        raw_q * gain_one,
+        raw_k * gain_one,
+        raw_v * gain_one,
+        out_grad,
+        grad_gain_two,
+        raw_gate * gain_two,
+        raw_up * gain_two,
+        down_sum.astype(f32),
+    )
+
+
 def solution(mesh):
     placed = (
         P("seq", "ctx", None),
@@ -368,8 +944,10 @@
         P("seq", None),
         P("seq", None),
     )
+    fits = mesh.shape["ctx"] == H and mesh.shape["seq"] == 4
+    chosen = ring_device if fits else general_device
     return jax.shard_map(
-        per_device,
+        chosen,
         mesh=mesh,
         in_specs=placed,
         out_specs=(

time: 3750 us -> 877 us (0.23)
  waiting for transfers between devices: 3330 us -> 0 us
  Pallas kernels: 0 us -> 689 us
  matrix products: 244 us -> 108 us
  blocking collectives: 48.3 us -> 0 us
  local copies, waits for them, and re-layouts: 69.7 us -> 24.1 us
    reduce_scatter x16 -> x0, waiting for transfers between devices: 2400 us -> none  [the longest x3 1180 us: reduce_grads(): lax.psum_scatter(grad_three.astype(jnp.bfloat16), 'ctx', scatter_dimensio...]
    all_gather x9 -> x0, waiting for transfers between devices: 814 us -> none  [the longest x1 191 us: mlp_weights(): lax.all_gather(w_gate, ('seq', 'ctx'), axis=0, tiled=True)]
    pallas_call x0 -> x7, Pallas kernels: none -> 689 us  [call(): pl.pallas_call(body, out_shape=outs, in_specs=[pl.BlockSpec(memory_space=...]
    unnamed x29 -> x0, waiting for transfers between devices: 113 us -> none
    dot_general x25 -> x6, matrix products: 108 us -> 34.7 us  [the longest x1 14.9 us: ring_device(): gu = jnp.dot(h_all, wcol_all, preferred_element_type=f32)]
    unnamed x2 -> x0, blocking collectives: 48.3 us -> none
    dot_general x7 -> x6, matrix products: 76 us -> 41.3 us  [contract_cols(): lax.dot_general(first_mat, second_mat, (((1,), (1,)), ((), ())), preferre...]
  transfers between devices with their start and end apart: 27 -> 0, of which waited for: 27 -> 0; matrix products, arithmetic and copies ran while one was open for 6% -> 0% of each run, Pallas kernels for 0% -> 0%
where the time goes in v1:
time: 877 us; the launch traced here: 868 us
  Pallas kernels  689 us (79%)
  matrix products  108 us (12%)
  other arithmetic  44.6 us (5%)
  local copies, waits for them, and re-layouts  24.1 us (3%)
    pallas_call x7, Pallas kernels, call(): pl.pallas_call(body, out_shape=outs, in_specs=[pl.BlockSpec(memory_space=...  689 us
    dot_general x6, matrix products, contract_cols(): lax.dot_general(first_mat, second_mat, (((1,), (1,)), ((), ())), preferre...  41.3 us
    dot_general x6, matrix products, contract_rows(): lax.dot_general(first_mat, second_mat, (((0,), (0,)), ((), ())), preferre...  31.8 us

profile of v1, /device:TPU:0, one launch (start us, length us, event | category | flops | bytes accessed | tf_op | source)
XLA Modules:
  0.0 867.5 jit_solution(14223913643988222072)
XLA Ops:
  0.7 0.8 convert_element_type.123
  1.5 0.7 convert_element_type.133
  2.8 0.7 pad_add_fusion
  3.4 1.2 fusion.8
  6.0 1.3 reduce.3
  8.3 1.2 fusion.33
  9.5 1.1 fusion.52
  10.6 0.9 maximum_bitcast_fusion.wqkv
  11.6 0.9 fusion.9.x
  13.7 1.5 reshape.307
  15.9 1.5 reshape.309
  17.4 2.8 pad_maximum_fusion.3.wcol
  20.2 140.1 %shard_map.212 = (bf16[8,128,2048]{2,1,0:T(8,128)(2,1)}, bf16[4,8,64,768]{3,2,1,0:T(8,128)(2,1)}, bf16[4,8,64,2048]{3,2,1,0:T(8,128)(2,1)}) custom-call(bf16[128,2048]{1,0:T(8,128)(2,1)} %fusion.9.x, bf16[8,64,768]{2,1,0:T(8,128)(2,1)} %maximum_bitcast_fusion.wqkv, bf16[64,2048]{1,0:T(8,128)(2,1)} %wout.1), custom_call_target="tpu_custom_call" | custom-call | tf_op jit(solution)/shard_map/pallas_call | solution.py:571
  160.3 6.2 fusion.73
  166.5 2.4 fusion.36
  169.0 1.2 fusion.72
  170.9 1.7 convolution_convert_fusion.9
  172.6 132.5 %shard_map.213 = (bf16[8,128,256]{2,1,0:T(8,128)(2,1)}, bf16[8,128,2048]{2,1,0:T(8,128)(2,1)}, bf16[4,8,64,2048]{3,2,1,0:T(8,128)(2,1)}, bf16[4,256,2048]{2,1,0:T(8,128)(2,1)}) custom-call(bf16[8,128,256]{2,1,0:T(8,128)(2,1)} %bitcast.155, bf16[128,2048]{1,0:T(8,128)(2,1)} %bitcast.139, bf16[8,64,2048]{2,1,0:T(8,128)(2,1)} %pad_maximum_fusion.3.wcol, ...), custom_call_target="tpu_custom_call" | custom-call | tf_op jit(solution)/shard_map/pallas_call | solution.py:571
  305.1 1.3 copy.71
  306.4 4.7 multiply_reduce_fusion.2
  311.2 0.9 multiply_convert_fusion.4.x
  312.1 43.8 %shard_map.214 = bf16[8,128,2048]{2,1,0:T(8,128)(2,1)} custom-call(bf16[128,2048]{1,0:T(8,128)(2,1)} %multiply_convert_fusion.4.x), custom_call_target="tpu_custom_call" | custom-call | tf_op jit(solution)/shard_map/pallas_call | solution.py:571
  355.9 14.9 %fusion.74 = f32[1024,2048]{0,1:T(8,128)} fusion(bf16[1024,2048]{1,0:T(8,128)(2,1)} %bitcast.126, bf16[2048,2048]{1,0:T(8,128)(2,1)} %bitcast.157), kind=kOutput, calls=%fused_computation.151 | convolution fusion | flops 8589934592 | bytes 20971520 | tf_op jit(solution)/shard_map/dot_general | solution.py:816
  370.9 9.7 %multiply_convert_fusion.3 = (bf16[1024,1024]{0,1:T(8,128)(2,1)}, bf16[1024,1024]{0,1:T(8,128)(2,1)}, bf16[1024,1024]{0,1:T(8,128)(2,1)S(1)}) fusion(f32[1024,2048]{0,1:T(8,128)} %fusion.74, bf16[1024,2048]{1,0:T(8,128)(2,1)S(1)} %bitcast.163, bf16[1024,2048]{1,0:T(8,128)(2,1)S(1)} %bitcast.161), kind=kOutput, calls=%fused_computation.8 | convolution fusion | flops 4310695936 | bytes 23068672 | tf_op jit(solution)/shard_map/dot_general | solution.py:65
  380.6 15.1 %convolution_convert_fusion.2 = bf16[1024,2048]{1,0:T(8,128)(2,1)} fusion(bf16[2048,2048]{1,0:T(8,128)(2,1)} %bitcast.158, bf16[1024,1024]{0,1:T(8,128)(2,1)} %get-tuple-element.40, bf16[1024,1024]{0,1:T(8,128)(2,1)} %get-tuple-element.39), kind=kOutput, calls=%fused_computation.13 | convolution fusion | flops 8600420352 | bytes 16777216 | tf_op jit(solution)/shard_map/dot_general | solution.py:65
  395.7 13.4 %convolution_convert_fusion = bf16[2048,2048]{1,0:T(8,128)(2,1)} fusion(bf16[1024,2048]{1,0:T(8,128)(2,1)S(1)} %bitcast.127, bf16[1024,1024]{0,1:T(8,128)(2,1)} %get-tuple-element.40, bf16[1024,1024]{0,1:T(8,128)(2,1)} %get-tuple-element.39), kind=kOutput, calls=%fused_computation.1 | convolution fusion | flops 8602517504 | bytes 16777216 | tf_op jit(solution)/shard_map/dot_general | solution.py:59
  409.2 6.1 convolution_convert_fusion.4
  415.2 6.4 convolution_convert_fusion.5
  421.6 87.3 %shard_map.215 = (f32[128,2048]{1,0:T(8,128)}, f32[128,2048]{1,0:T(8,128)}) custom-call(bf16[8,128,2048]{2,1,0:T(8,128)(2,1)} %bitcast.128, bf16[8,128,2048]{2,1,0:T(8,128)(2,1)} %bitcast.129), custom_call_target="tpu_custom_call" | custom-call | tf_op jit(solution)/shard_map/pallas_call | solution.py:571
  508.9 1.4 multiply_reduce_fusion.1
  510.4 2.7 subtract_add_fusion
  513.0 6.3 convolution_convert_fusion.7
  519.5 1.0 copy.75
  520.6 9.8 %shard_map.216 = bf16[8,128,256]{2,1,0:T(8,128)(2,1)} custom-call(bf16[8,128,256]{2,1,0:T(8,128)(2,1)} %bitcast.138), custom_call_target="tpu_custom_call" | custom-call | tf_op jit(solution)/shard_map/pallas_call | solution.py:571
  530.4 3.9 multiply_reduce_fusion
  534.4 1.2 multiply_convert_fusion
  535.6 0.7 convolution_multiply_fusion.1
  536.5 0.7 convolution_multiply_fusion
  537.3 2.3 fusion.59
  539.5 2.3 fusion.58
  541.8 2.5 fusion.57
  544.3 2.3 fusion.56
  546.6 1.0 fusion.7
  547.6 1.1 copy-done.32
  548.7 4.9 convolution_convert_fusion.6
  553.6 5.1 convolution_convert_fusion.3
  558.7 45.1 %shard_map.217 = f32[128,2048]{1,0:T(8,128)} custom-call(bf16[8,128,2048]{2,1,0:T(8,128)(2,1)} %bitcast.123), custom_call_target="tpu_custom_call" | custom-call | tf_op jit(solution)/shard_map/pallas_call | solution.py:571
  603.8 1.4 fusion.14
  605.2 2.6 fusion.13
  607.8 5.6 convolution_convert_fusion.1
  613.4 230.7 %shard_map.218 = (bf16[8,64,2048]{2,1,0:T(8,128)(2,1)}, bf16[256,2048]{1,0:T(8,128)(2,1)}, bf16[8,64,768]{2,1,0:T(8,128)(2,1)}, f32[64,2048]{1,0:T(8,128)}) custom-call(bf16[4,512,2048]{2,1,0:T(8,128)(2,1)} %bitcast.116, bf16[4,256,2048]{2,1,0:T(8,128)(2,1)} %bitcast.134, bf16[4,512,768]{2,1,0:T(8,128)(2,1)} %bitcast.135, bf16[4,512,2048]{2,1,0:T(8,128)(2,1)} %bitcast.113), custom_call_target="tpu_custom_call" | custom-call | tf_op jit(solution)/shard_map/pallas_call | solution.py:571
  844.1 1.3 convert_element_type.153
  845.7 1.0 broadcast_multiply_fusion.2
  846.8 1.0 broadcast_multiply_fusion.3
  848.3 1.6 convert_element_type.155
  849.9 2.5 fusion.71
  852.3 2.2 reshape.332
  854.5 1.2 copy.80
  855.8 2.5 copy.91
  858.3 2.2 reshape.330
  860.5 1.2 copy.79
  861.8 1.2 copy.90
  863.0 2.8 broadcast_multiply_fusion
  866.3 0.8 copy.107
  (113 shorter events, 7.2 us)
Async XLA Ops:
  0.6 10.9 %copy-start.2 = (bf16[1,128,2048]{2,1,0:T(8,128)(2,1)S(1)}, bf16[1,128,2048]{2,1,0:T(8,128)(2,1)}, u32[]{:S(2)}) copy-start(bf16[1,128,2048]{2,1,0:T(8,128)(2,1)} %param.13) | copy-start | bytes 1572868
  0.7 11.9 %copy-start.7 = (bf16[64,8192]{1,0:T(8,128)(2,1)S(1)}, bf16[64,8192]{1,0:T(8,128)(2,1)}, u32[]{:S(2)}) copy-start(bf16[64,8192]{1,0:T(8,128)(2,1)} %param.21) | copy-start | bytes 3145732
  1.5 11.5 %copy-start.25 = (f32[64]{0:T(128)}, f32[64]{0:T(128)S(1)}, u32[]{:S(2)}) copy-start(f32[64]{0:T(128)S(1)} %convert_element_type.123) | copy-start | bytes 772
  2.1 10.8 %copy-start.27 = (f32[64]{0:T(128)}, f32[64]{0:T(128)S(1)}, u32[]{:S(2)}) copy-start(f32[64]{0:T(128)S(1)} %convert_element_type.133) | copy-start | bytes 772
  5.2 7.8 copy-start.29
  8.3 4.3 copy-start.9
  15.2 2.2 copy-start.6
  166.5 4.4 copy-start.12
  168.9 1.3 copy-start.19
  169.0 1.3 copy-start.21
  169.0 1.3 copy-start.23
  170.2 2.4 copy-start
  355.9 14.9 %copy-start.33 = (bf16[4,256,2048]{2,1,0:T(8,128)(2,1)S(1)}, bf16[4,256,2048]{2,1,0:T(8,128)(2,1)}, u32[]{:S(2)}) copy-start(bf16[4,256,2048]{2,1,0:T(8,128)(2,1)} %get-tuple-element.29) | copy-start | bytes 12582916
  355.9 14.9 %copy-start.34 = (bf16[8,128,2048]{2,1,0:T(8,128)(2,1)S(1)}, bf16[8,128,2048]{2,1,0:T(8,128)(2,1)}, u32[]{:S(2)}) copy-start(bf16[8,128,2048]{2,1,0:T(8,128)(2,1)} %get-tuple-element.28) | copy-start | bytes 12582916
  380.6 15.1 %copy-start.5 = (bf16[8,128,2048]{2,1,0:T(8,128)(2,1)S(1)}, bf16[8,128,2048]{2,1,0:T(8,128)(2,1)}, u32[]{:S(2)}) copy-start(bf16[8,128,2048]{2,1,0:T(8,128)(2,1)} %shard_map.214) | copy-start | bytes 12582916
  395.7 13.5 %copy-start.35 = (bf16[8,128,2048]{2,1,0:T(8,128)(2,1)S(1)}, bf16[8,128,2048]{2,1,0:T(8,128)(2,1)}, u32[]{:S(2)}) copy-start(bf16[8,128,2048]{2,1,0:T(8,128)(2,1)} %get-tuple-element.28) | copy-start | bytes 12582916
  421.6 88.7 %copy-start.11 = (bf16[1,128,2048]{2,1,0:T(8,128)(2,1)S(1)}, bf16[1,128,2048]{2,1,0:T(8,128)(2,1)}, u32[]{:S(2)}) copy-start(bf16[1,128,2048]{2,1,0:T(8,128)(2,1)} %param.14) | copy-start | bytes 1572868
  530.4 4.0 copy-start.1
  534.4 1.2 copy-start.22
  534.4 1.2 copy-start.24
  535.6 1.0 copy-start.20
  536.5 10.0 %copy-start.16 = (bf16[8,128,256]{2,1,0:T(8,128)(2,1)S(1)}, bf16[8,128,256]{2,1,0:T(8,128)(2,1)}, u32[]{:S(2)}) copy-start(bf16[8,128,256]{2,1,0:T(8,128)(2,1)} %shard_map.216) | copy-start | bytes 1572868
  546.5 2.2 copy-start.32
  548.7 4.9 copy-start.36
  558.7 46.5 %copy-start.30 = (f32[128]{0:T(128)S(1)}, f32[128]{0:T(128)}, u32[]{:S(2)}) copy-start(f32[128]{0:T(128)} %copy-done.29) | copy-start | bytes 1540
  558.7 46.5 %copy-start.31 = (f32[128]{0:T(128)S(1)}, f32[128]{0:T(128)}, u32[]{:S(2)}) copy-start(f32[128]{0:T(128)} %get-tuple-element.64) | copy-start | bytes 1540
  844.1 1.6 copy-start.14
  844.1 1.6 copy-start.26
  844.1 2.6 copy-start.17
  844.1 2.6 copy-start.18
  845.5 2.8 copy-start.13
  845.6 4.2 copy-start.3
  860.5 2.5 copy-start.4
  860.5 2.5 copy-start.8
  860.5 2.5 copy-start.10
  860.5 2.5 copy-start.28
  863.0 3.3 copy-start.15

commit v2 on v1

--- a/solution.py
+++ b/solution.py
@@ -410,7 +410,33 @@
     return [pltpu.SemaphoreType.DMA((2, RING // 2, 2))] * 2
 
 
-def ring_gather(own, buf, sems, place):
+def slot(offset):
+    return 0 if offset == 0 else min(RING - 1, 2 * offset if offset > 0 else -2 * offset - 1)
+
+
+class Rows:
+    def __init__(self, ref, rows):
+        self.ref, self.rows = ref, rows
+
+    def here(self, offset):
+        return self.ref.at[pl.ds(slot(offset) * self.rows, self.rows)]
+
+    def there(self, offset, d):
+        return self.here(offset - 1 if d == 0 else offset + 1)
+
+
+class Owners:
+    def __init__(self, ref, place):
+        self.ref, self.place = ref, place
+
+    def here(self, offset):
+        return self.ref.at[self.place.at(offset)]
+
+    def there(self, offset, d):
+        return self.here(offset)
+
+
+def ring_gather(own, blocks, sems, place):
     half = own.shape[0] // 2
     steps = RING // 2
     sent = []
@@ -418,11 +444,9 @@
     def part(ref, j):
         return ref.at[pl.ds(j * half, half)]
 
-    def owner(d, s):
-        return place.at(-s if d == 0 else s)
-
     def wait_for(d, s, j):
-        arrived(part(buf.at[owner(d, s + 1)], j), sems, (d, s, j), place.right if d == 0 else place.left)
+        offset = -(s + 1) if d == 0 else s + 1
+        arrived(part(blocks.here(offset), j), sems, (d, s, j), place.right if d == 0 else place.left)
 
     for s in range(steps):
         for j in range(2):
@@ -431,9 +455,10 @@
                     continue
                 if s > 0:
                     wait_for(d, s - 1, j)
+                offset = -s if d == 0 else s
                 copy = remote(
-                    part(own if s == 0 else buf.at[owner(d, s)], j),
-                    part(buf.at[owner(d, s)], j),
+                    part(own if s == 0 else blocks.here(offset), j),
+                    part(blocks.there(offset, d), j),
                     sems[0].at[d, s, j],
                     sems[1].at[d, s, j],
                     place.right if d == 0 else place.left,
@@ -443,71 +468,101 @@
             yield
     for d in range(2):
         wait_for(d, steps - 2, 1 - d)
+    yield
+    for d in range(2):
         wait_for(d, steps - 1, d)
-        yield
+    yield
     for copy in sent:
         copy.wait_send()
 
 
-def ring_scatter(part, out, slots, sems, place):
-    half = part.shape[1] // 2
-    steps = RING // 2
-    sent = []
-
-    def rows(ref, j):
-        return ref.at[pl.ds(j * half, half)]
-
-    def block(d, s):
-        return place.at(steps - s if d == 0 else s - steps)
-
-    def side(d):
-        return place.right if d == 0 else place.left
-
-    for s in range(steps):
+class RingSum:
+    def __init__(self, slots, sems, place):
+        self.slots, self.sems, self.sent = slots, sems, []
+        self.sides = (place.right, place.left)
+        self.half = slots.shape[2] // 2
+
+    def rows(self, ref, j):
+        return ref.at[pl.ds(j * self.half, self.half)]
+
+    def send(self, d, s, j, source):
+        to = self.rows(self.slots.at[d, s], j)
+        copy = remote(source, to, self.sems[0].at[d, s, j], self.sems[1].at[d, s, j], self.sides[d])
+        copy.start()
+        self.sent.append(copy)
+
+    def held(self, d, s, j):
+        ref = self.rows(self.slots.at[d, s], j)
+        arrived(ref, self.sems, (d, s, j), self.sides[d])
+        return ref
+
+    def first(self, part):
+        for d in range(2):
+            self.send(d, 0, d, self.rows(part, d))
+
+    def relay(self, s, parts):
         for j in range(2):
             for d in range(2):
-                if s == 0 and j != d:
-                    continue
-                source = rows(part.at[block(d, s)], j)
-                if s > 1 or (s == 1 and j == d):
-                    held = rows(slots.at[d, s - 1], j)
-                    arrived(held, sems, (d, s - 1, j), side(d))
-                    held[...] = (held[...].astype(jnp.float32) + source[...].astype(jnp.float32)).astype(held.dtype)
+                source = self.rows(parts[d], j)
+                if s > 1 or j == d:
+                    held = self.held(d, s - 1, j)
+                    add_into(held, source)
                     source = held
-                copy = remote(source, rows(slots.at[d, s], j), sems[0].at[d, s, j], sems[1].at[d, s, j], side(d))
-                copy.start()
-                sent.append(copy)
-            yield
-    for j in range(2):
-        total = rows(part.at[place.c], j)[...].astype(jnp.float32)
-        for d in range(2):
-            held = rows(slots.at[d, steps - 1], j)
-            arrived(held, sems, (d, steps - 1, j), side(d))
-            total = total + held[...].astype(jnp.float32)
-        rows(out, j)[...] = total
+                self.send(d, s, j, source)
+
+    def last(self, part, out):
+        for j in range(2):
+            held = [self.held(d, RING // 2 - 1, j) for d in range(2)]
+            sum_of_three(self.rows(out, j), self.rows(part, j), *held)
+
+    def end(self):
+        for copy in self.sent:
+            copy.wait_send()
+
+
+def ring_scatter(blocks, out, slots, sems, place):
+    ring = RingSum(slots, sems, place)
+    ring.first(blocks.here(RING // 2))
+    yield
+    for s in range(1, RING // 2):
+        k = RING // 2 - s
+        ring.relay(s, (blocks.here(k), blocks.here(-k)))
         yield
+    ring.last(blocks.here(0), out)
+    ring.end()
+    yield
+
+
+def pair_sems():
+    return [pltpu.SemaphoreType.DMA((RING,))] * 2
+
+
+OFFSETS = (1, -1, 2, -2, 3, -3, 4)
+
+
+def exchange(send, there, here, sems, place):
+    sent = []
+    for k in OFFSETS:
+        at = slot(k)
+        copy = remote(send(k), there(k), sems[0].at[at], sems[1].at[at], {"ctx": place.at(k)})
+        copy.start()
+        sent.append(copy)
+    yield
+    for k in OFFSETS:
+        arrived(here(k), sems, slot(-k) if k != RING // 2 else RING - 1, {"ctx": place.at(k)})
     for copy in sent:
         copy.wait_send()
-
-
-def pair_sems():
-    return [pltpu.SemaphoreType.DMA((RING,))] * 2
-
-
-def exchange(src, buf, sems, place):
-    sent = []
-    for k in range(1, RING):
-        to = lax.rem(place.c + k, RING)
-        copy = remote(src.at[to], buf.at[place.c], sems[0].at[k], sems[1].at[k], {"ctx": to})
-        copy.start()
-        sent.append(copy)
-    yield
-    for k in range(1, RING):
-        source = lax.rem(place.c + RING - k, RING)
-        arrived(buf.at[source], sems, k, {"ctx": source})
-    for copy in sent:
-        copy.wait_send()
-    yield
+    yield
+
+
+def by_owner(src, dst, sems, place):
+    return exchange(
+        lambda k: src.at[place.at(k)], lambda k: dst.at[place.c], lambda k: dst.at[place.at(k)], sems, place
+    )
+
+
+def pairs_of(sems):
+    return [sems[i : i + 2] for i in range(0, len(sems), 2)]
 
 
 def seq_sems():
@@ -531,9 +586,19 @@
     yield
 
 
+def sum_of_three(dst, *terms):
+    step = math.gcd(dst.shape[0], 16)
+
+    @pl.loop(0, dst.shape[0] // step)
+    def _(i):
+        at = pl.ds(pl.multiple_of(i * step, step), step)
+        one, two, three = (term[at].astype(jnp.float32) for term in terms)
+        dst[at] = one + two + three
+
+
 def add_into(dst, other):
     rows = dst.shape[0]
-    step = math.gcd(rows, 32)
+    step = math.gcd(rows, 16)
 
     @pl.loop(0, rows // step)
     def _(i):
@@ -575,7 +640,7 @@
         out_specs=[pl.BlockSpec(memory_space=space) for space in out_spaces],
         scratch_shapes=scratch,
         compiler_params=pltpu.CompilerParams(
-            collective_id=ident, has_side_effects=True, vmem_limit_bytes=56 * 1024 * 1024
+            collective_id=ident, has_side_effects=True, vmem_limit_bytes=63 * 1024 * 1024
         ),
     )(*args)
 
@@ -584,119 +649,289 @@
     return jax.ShapeDtypeStruct(shape, dtype)
 
 
-def start_kernel(x, wqkv, wout, x_all, wqkv_all, wout_all, local, r0, r1, e0, e1, q0, q1, o0, o1, w0, w1):
+def attention_in_kernel(x, wqkv, wout, x_all, wqkv_all, wout_all, local, *sems):
     place = Place()
+    x_ring, qkv_swap, qkv_seq, out_ring, out_seq = pairs_of(sems)
     greet(place.peers() + [place.core_peer, place.far_peer])
+    x_blocks = Rows(x_all, x.shape[0])
     keep = [
-        pltpu.make_async_copy(x, x_all.at[place.c], local.at[0]),
+        pltpu.make_async_copy(x, x_blocks.here(0), local.at[0]),
         pltpu.make_async_copy(wqkv.at[place.c], wqkv_all.at[place.s, place.c], local.at[1]),
         pltpu.make_async_copy(wout, wout_all.at[place.s, place.c], local.at[2]),
     ]
     for copy in keep:
         copy.start()
 
-    def attention_weights_flow():
-        yield from exchange(wqkv, wqkv_all.at[place.s], (e0, e1), place)
+    def qkv_flow():
+        yield from by_owner(wqkv, wqkv_all.at[place.s], qkv_swap, place)
         keep[1].wait()
-        yield from seq_gather(wqkv_all.at[place.s], wqkv_all, (q0, q1), place)
-
-    together(attention_weights_flow(), ring_gather(x, x_all, (r0, r1), place))
-
-    def out_weights_flow():
-        yield from ring_gather(wout, wout_all.at[place.s], (o0, o1), place)
+        yield from seq_gather(wqkv_all.at[place.s], wqkv_all, qkv_seq, place)
+
+    def out_flow():
+        yield from ring_gather(wout, Owners(wout_all.at[place.s], place), out_ring, place)
         keep[2].wait()
-        yield from seq_gather(wout_all.at[place.s], wout_all, (w0, w1), place)
-
-    together(out_weights_flow())
+        yield from seq_gather(wout_all.at[place.s], wout_all, out_seq, place)
+
+    first, second, third = qkv_flow(), out_flow(), ring_gather(x, x_blocks, x_ring, place)
+    next(first)
+    for _ in range(RING):
+        next(second)
+    next(first)
+    together(third, first, second)
     keep[0].wait()
 
 
-def middle_kernel(ob, dy, wcol, wdown, ob_all, dy_all, wcol_all, wdown_all, local, a0, a1, r0, r1, e0, e1, q0, q1, w0, w1):
+def attention_out_kernel(ob, dy, wcol, wdown, ob_all, dy_all, wcol_all, wdown_all, local, *sems):
     place = Place()
+    ob_swap, dy_ring, gate_swap, gate_seq, up_swap, up_seq, down_seq = pairs_of(sems)
     greet(place.peers() + [place.core_peer, place.far_peer])
+    ob_blocks, dy_blocks = Rows(ob, dy.shape[0]), Rows(dy_all, dy.shape[0])
     keep = [
-        pltpu.make_async_copy(ob.at[place.c], ob_all.at[place.c], local.at[0]),
-        pltpu.make_async_copy(dy, dy_all.at[place.c], local.at[1]),
-        pltpu.make_async_copy(wcol.at[place.c], wcol_all.at[place.s, place.c], local.at[2]),
-        pltpu.make_async_copy(wdown, wdown_all.at[place.s], local.at[3]),
+        pltpu.make_async_copy(ob_blocks.here(0), ob_all.at[place.c], local.at[0]),
+        pltpu.make_async_copy(dy, dy_blocks.here(0), local.at[1]),
+        pltpu.make_async_copy(wcol.at[0, place.c], wcol_all.at[0, place.s, place.c], local.at[2]),
+        pltpu.make_async_copy(wcol.at[1, place.c], wcol_all.at[1, place.s, place.c], local.at[3]),
+        pltpu.make_async_copy(wdown, wdown_all.at[place.s], local.at[4]),
     ]
     for copy in keep:
         copy.start()
 
-    def columns_flow():
-        yield from exchange(wcol, wcol_all.at[place.s], (e0, e1), place)
-        keep[2].wait()
-        yield from seq_gather(wcol_all.at[place.s], wcol_all, (q0, q1), place)
-
-    together(
-        exchange(ob, ob_all, (a0, a1), place),
-        columns_flow(),
-        seq_gather(wdown, wdown_all, (w0, w1), place),
-        ring_gather(dy, dy_all, (r0, r1), place),
-    )
+    def columns_flow(i, swap, seq):
+        yield from by_owner(wcol.at[i], wcol_all.at[i, place.s], swap, place)
+        keep[2 + i].wait()
+        yield from seq_gather(wcol_all.at[i, place.s], wcol_all.at[i], seq, place)
+
+    ob_flow = exchange(ob_blocks.here, lambda k: ob_all.at[place.c], lambda k: ob_all.at[place.at(k)], ob_swap, place)
+    gate_flow, up_flow = columns_flow(0, gate_swap, gate_seq), columns_flow(1, up_swap, up_seq)
+    down_flow = seq_gather(wdown, wdown_all, down_seq, place)
+    next(ob_flow)
+    next(gate_flow)
+    next(down_flow)
+    next(ob_flow)
+    next(gate_flow)
+    next(up_flow)
+    next(gate_flow)
+    together(up_flow, ring_gather(dy, dy_blocks, dy_ring, place), gate_flow, ob_flow, down_flow)
     keep[0].wait()
     keep[1].wait()
-    keep[3].wait()
-
-
-def gather_kernel(x, x_all, local, r0, r1):
+    keep[4].wait()
+
+
+def dot(a, b, at=(1, 0)):
+    return lax.dot_general(a, b, (((at[0],), (at[1],)), ((), ())), preferred_element_type=jnp.float32)
+
+
+def chunks(total, size, body):
+    @pl.loop(0, total // size)
+    def _(i):
+        body(pl.ds(pl.multiple_of(i * size, size), size))
+
+
+def mlp_kernel(hhat, dy_hbm, wcol_hbm, wdown_hbm, sum_h, sum_o, col_out, down_out,
+               h_all, dy_all, wg, wu, wd, mid, dgate, dup, stage_h, stage_o, stage, slots_h, slots_o,
+               col_sent, col_near, col_far, down_sent, down_near, down_far, local, *sems):
     place = Place()
-    greet([place.right, place.left])
-    keep = pltpu.make_async_copy(x, x_all.at[place.c], local)
-    keep.start()
-    together(ring_gather(x, x_all, (r0, r1), place))
-    keep.wait()
-
-
-def scatter_kernel(count, *refs):
-    parts, outs, slots, sems = refs[:count], refs[count : 2 * count], refs[2 * count : 3 * count], refs[3 * count :]
-    place = Place()
-    greet([place.right, place.left])
-    for i in range(count):
-        together(ring_scatter(parts[i], outs[i], slots[i], sems[2 * i : 2 * i + 2], place))
-
-
-def swap_kernel(x, x_all, local, a0, a1):
+    h_sems, sum_h_sems, sum_o_sems, col_seq, down_seq = pairs_of(sems)
+    greet([place.right, place.left, place.core_peer, place.far_peer])
+    rows, width = hhat.shape
+    ff = wg.shape[1]
+    bf16, f32 = jnp.bfloat16, jnp.float32
+    keep = [
+        pltpu.make_async_copy(src, dst, local.at[i])
+        for i, (src, dst) in enumerate(
+            ((hhat, h_all.at[pl.ds(0, rows)]), (wcol_hbm.at[0], wg), (wcol_hbm.at[1], wu), (wdown_hbm, wd), (dy_hbm, dy_all))
+        )
+    ]
+    for copy in keep:
+        copy.start()
+    gather = ring_gather(hhat, Rows(h_all, rows), h_sems, place)
+    next(gather)
+    next(gather)
+    for copy in keep:
+        copy.wait()
+
+    def hidden_rows(start, count):
+        at = pl.ds(start, count)
+
+        def body(cols):
+            gate = dot(h_all[at, :], wg[:, cols])
+            up = dot(h_all[at, :], wu[:, cols])
+            dmid = dot(dy_all[at, :], wd[cols, :], (1, 1))
+            sig = jax.nn.sigmoid(gate)
+            active = gate * sig
+            mid[at, cols] = (active * up).astype(bf16)
+            dgate[at, cols] = (dmid * up * sig * (1.0 + gate * (1.0 - sig))).astype(bf16)
+            dup[at, cols] = (dmid * active).astype(bf16)
+
+        chunks(ff, 256, body)
+
+    def part_h(start, count, dst):
+        at = pl.ds(start, count)
+
+        def body(cols):
+            dst[:, cols] = (dot(dgate[at, :], wg[cols, :], (1, 1)) + dot(dup[at, :], wu[cols, :], (1, 1))).astype(bf16)
+
+        chunks(width, 256, body)
+
+    def part_o(start, count, dst):
+        at = pl.ds(start, count)
+
+        def body(cols):
+            dst[:, cols] = dot(mid[at, :], wd[:, cols]).astype(bf16)
+
+        chunks(width, 256, body)
+
+    def col_grad(s, dst, add):
+        def body(cols):
+            lhs = h_all[:, pl.ds(pl.multiple_of(s * dst.shape[0] + cols.start, 256), 256)]
+            for side, grad in enumerate((dgate, dup)):
+                there = pl.ds(side * ff, ff)
+                value = dot(lhs, grad[...], (0, 0))
+                if add:
+                    value = value + dst[cols, there].astype(f32)
+                dst[cols, there] = value.astype(bf16)
+
+        chunks(dst.shape[0], 256, body)
+
+    def down_grad(s, dst, add):
+        lhs = pl.ds(pl.multiple_of(s * dst.shape[0], 256), dst.shape[0])
+
+        def body(cols):
+            value = dot(mid[:, lhs], dy_all[:, cols], (0, 0))
+            if add:
+                value = value + dst[:, cols].astype(f32)
+            dst[:, cols] = value.astype(bf16)
+
+        chunks(width, 512, body)
+
+    hidden_rows(0, rows)
+    for k in range(1, 4):
+        next(gather)
+        if k < 3:
+            next(gather)
+        else:
+            next(gather)
+            next(gather)
+        hidden_rows((2 * k - 1) * rows, 2 * rows)
+    next(gather)
+    hidden_rows(7 * rows, rows)
+
+    def pair(ref):
+        return (ref.at[pl.ds(rows, rows)], ref.at[pl.ds(0, rows)])
+
+    low, row = lax.rem(place.s, 2), place.s // 2
+    other_row = 1 - row
+    sent = []
+
+    def near_send(i, grad, source, near, seq):
+        r = (other_row, row)[i]
+        grad(r * 2 + 1 - low, source.at[i], False)
+        copy = remote(source.at[i], near.at[i], seq[0].at[i], seq[1].at[i], place.core_peer)
+        copy.start()
+        sent.append(copy)
+
+    def far_send(grad, near, far, seq):
+        arrived(near.at[0], seq, 0, place.core_peer)
+        grad(other_row * 2 + low, near.at[0], True)
+        copy = remote(near.at[0], far, seq[0].at[2], seq[1].at[2], place.far_peer)
+        copy.start()
+        sent.append(copy)
+
+    def own_sum(grad, near, seq):
+        arrived(near.at[1], seq, 1, place.core_peer)
+        grad(row * 2 + low, near.at[1], True)
+
+    def far_sum(near, far, seq, out, sem):
+        arrived(far, seq, 2, place.far_peer)
+        add_into(far, near.at[1])
+        copy = pltpu.make_async_copy(far, out, sem)
+        copy.start()
+        return copy
+
+    ring_h, ring_o = RingSum(slots_h, sum_h_sems, place), RingSum(slots_o, sum_o_sems, place)
+    top_h, top_o = stage_h.at[pl.ds(2 * rows, rows)], stage_o.at[pl.ds(2 * rows, rows)]
+    next_h, next_o = stage_h.at[pl.ds(0, 2 * rows)], stage_o.at[pl.ds(0, 2 * rows)]
+    part_h(7 * rows, rows, top_h)
+    ring_h.first(top_h)
+    near_send(0, col_grad, col_sent, col_near, col_seq)
+    part_h(5 * rows, 2 * rows, next_h)
+    ring_h.relay(1, pair(next_h))
+    near_send(1, col_grad, col_sent, col_near, col_seq)
+    far_send(col_grad, col_near, col_far, col_seq)
+    part_o(7 * rows, rows, top_o)
+    ring_o.first(top_o)
+    part_h(3 * rows, 2 * rows, stage)
+    ring_h.relay(2, pair(stage))
+    part_o(5 * rows, 2 * rows, next_o)
+    ring_o.relay(1, pair(next_o))
+    near_send(0, down_grad, down_sent, down_near, down_seq)
+    part_h(rows, 2 * rows, stage)
+    ring_h.relay(3, pair(stage))
+    near_send(1, down_grad, down_sent, down_near, down_seq)
+    far_send(down_grad, down_near, down_far, down_seq)
+    part_o(3 * rows, 2 * rows, stage)
+    ring_o.relay(2, pair(stage))
+    own_sum(col_grad, col_near, col_seq)
+    part_h(0, rows, top_stage := stage.at[pl.ds(0, rows)])
+    ring_h.last(top_stage, sum_h)
+    part_o(rows, 2 * rows, stage)
+    ring_o.relay(3, pair(stage))
+    own_sum(down_grad, down_near, down_seq)
+    part_o(0, rows, top_stage)
+    ring_o.last(top_stage, sum_o)
+    ends = [
+        far_sum(col_near, col_far, col_seq, col_out, local.at[0]),
+        far_sum(down_near, down_far, down_seq, down_out, local.at[1]),
+    ]
+    for copy in ends:
+        copy.wait()
+    ring_h.end()
+    ring_o.end()
+    for copy in sent:
+        copy.wait_send()
+    for _ in gather:
+        pass
+
+
+def swap_kernel(x, x_all, local, *sems):
     place = Place()
     greet(place.peers())
-    keep = pltpu.make_async_copy(x.at[place.c], x_all.at[place.c], local)
+    blocks = Rows(x_all, x.shape[1])
+    keep = pltpu.make_async_copy(x.at[place.c], blocks.here(0), local)
     keep.start()
-    together(exchange(x, x_all, (a0, a1), place))
+    together(
+        exchange(lambda k: x.at[place.at(k)], lambda k: blocks.here(-k), blocks.here, sems, place)
+    )
     keep.wait()
 
 
-def grads_kernel(col, down, qkv, out, col_out, down_out, qkv_out, out_out,
-                 cn, cf, dn, df, qn, qf, on, of, slots, local, c0, c1, d0, d1, k0, k1, u0, u1, e0, e1, f0, f1, g0, g1):
+def grads_kernel(part_x, col, qkv, out, sum_x, col_out, qkv_out, out_out,
+                 slots_x, qkv_near, qkv_far, out_near, out_far, slots_o, local, *sems):
     place = Place()
+    x_ring, col_swap, qkv_seq, qkv_swap, out_seq, out_ring = pairs_of(sems)
     greet(place.peers() + [place.core_peer, place.far_peer])
 
-    def col_flow():
-        yield from seq_scatter(col, cn, cf, (c0, c1), place)
-        ref = cf.at[0]
-        keep = pltpu.make_async_copy(ref.at[pl.ds(pl.multiple_of(place.c * 64, 64), 64)], col_out.at[place.c], local.at[0])
+    def swap_flow(blocks, into, swap, sem):
+        keep = pltpu.make_async_copy(blocks.at[place.c], into.at[place.c], sem)
         keep.start()
-        yield from exchange(Blocks(ref, 64), col_out, (e0, e1), place)
+        yield from by_owner(blocks, into, swap, place)
         keep.wait()
 
     def qkv_flow():
-        yield from seq_scatter(qkv, qn, qf, (k0, k1), place)
-        ref = qf.at[0]
-        keep = pltpu.make_async_copy(ref.at[pl.ds(pl.multiple_of(place.c * 64, 64), 64)], qkv_out.at[place.c], local.at[1])
-        keep.start()
-        yield from exchange(Blocks(ref, 64), qkv_out, (f0, f1), place)
-        keep.wait()
-
-    def down_flow():
-        yield from seq_scatter(down, dn, df, (d0, d1), place)
-        keep = pltpu.make_async_copy(df.at[0], down_out, local.at[2])
-        keep.start()
-        keep.wait()
+        yield from seq_scatter(qkv, qkv_near, qkv_far, qkv_seq, place)
+        yield from swap_flow(Blocks(qkv_far.at[0], qkv_out.shape[1]), qkv_out, qkv_swap, local.at[1])
 
     def out_flow():
-        yield from seq_scatter(out, on, of, (u0, u1), place)
-        yield from ring_scatter(Blocks(of.at[0], 64), out_out, slots, (g0, g1), place)
-
-    together(out_flow(), col_flow(), qkv_flow(), down_flow())
+        yield from seq_scatter(out, out_near, out_far, out_seq, place)
+        blocks = Owners(Blocks(out_far.at[0], out_out.shape[0]), place)
+        yield from ring_scatter(blocks, out_out, slots_o, out_ring, place)
+
+    together(
+        ring_scatter(Rows(part_x, sum_x.shape[0]), sum_x, slots_x, x_ring, place),
+        qkv_flow(),
+        out_flow(),
+        swap_flow(Blocks(col, col_out.shape[1]), col_out, col_swap, local.at[0]),
+    )
 
 
 class Blocks:
@@ -744,26 +979,30 @@
     def by_context(w):
         return (w * gain_two).astype(bf16).reshape(shard, SEQ, n, ff_own).transpose(2, 0, 1, 3).reshape(n, shard, ff_mine)
 
-    wcol = jnp.concatenate([by_context(wg), by_context(wu)], axis=-1)
+    wcol = jnp.stack([by_context(wg), by_context(wu)])
 
     inputs = tokens[0].astype(f32)
     scale_one = rms_scale(inputs)
     xhat = (inputs * scale_one).astype(bf16)
 
     x_all, wqkv_all, wout_all = call(
-        start_kernel,
-        [shaped((n, rows, width)), shaped((SEQ, n, shard, 3 * head)), shaped((SEQ, n, shard, width))],
+        attention_in_kernel,
+        [shaped((seq_len, width)), shaped((SEQ, n, shard, 3 * head)), shaped((SEQ, n, shard, width))],
         (xhat, wqkv, w_out),
         [HBM] * 3,
         [HBM] * 3,
         [DMA((3,))] + ring_sems() + pair_sems() + seq_sems() + ring_sems() + seq_sems(),
         0,
     )
-    x_all = x_all.reshape(seq_len, width)
     wqkv_all = wqkv_all.reshape(width, 3 * head)
     wout_all = wout_all.reshape(H * head, width)
 
-    block = pair_order[0]
+    z, x = c // 2, lax.rem(c, 2)
+    ring_at = z + x * (7 - 2 * z)
+    offsets = jnp.array([0, -1, 1, -2, 2, -3, 3, 4], jnp.int32)
+    q = lax.rem(ring_at + offsets + n, n)
+    order = 2 * q + (q // 4) * (15 - 4 * q)
+    block = jnp.take(pair_order[0], order)
     blocks = jnp.stack([block, 2 * n - 1 - block], axis=1).reshape(-1)
     pos = (blocks[:, None] * half_rows + jnp.arange(half_rows, dtype=jnp.int32)[None, :]).reshape(-1)
     doc = jnp.take(segments[0].reshape(2 * n, half_rows), blocks, axis=0).reshape(-1)
@@ -788,51 +1027,51 @@
     ob = jnp.dot(prob_low, v, preferred_element_type=f32).astype(bf16)
 
     ob_all, dy_all, wcol_all, wdown_all = call(
-        middle_kernel,
+        attention_out_kernel,
         [
             shaped((n, rows, head)),
-            shaped((n, rows, width)),
-            shaped((SEQ, n, shard, 2 * ff_mine)),
+            shaped((seq_len, width)),
+            shaped((2, SEQ, n, shard, ff_mine)),
             shaped((SEQ, ff_own, width)),
         ],
-        (ob.reshape(n, rows, head), cotangent[0], wcol, w_down),
+        (ob, cotangent[0], wcol, w_down),
         [HBM] * 4,
         [HBM] * 4,
-        [DMA((4,))] + pair_sems() + ring_sems() + pair_sems() + seq_sems() + seq_sems(),
+        [DMA((5,))] + pair_sems() + ring_sems() + (pair_sems() + seq_sems()) * 2 + seq_sems(),
         1,
     )
     ob_local = ob_all.transpose(1, 0, 2).reshape(rows, H * head)
-    dy_all = dy_all.reshape(seq_len, width)
-    wcol_all = wcol_all.reshape(width, 2 * ff_mine)
-    wdown_all = wdown_all.reshape(ff_mine, width)
+    wcol_all = wcol_all.reshape(2, width, ff_mine)
 
     hidden = inputs + jnp.dot(ob_local, wout_all, preferred_element_type=f32)
     scale_two = rms_scale(hidden)
     hhat = (hidden * scale_two).astype(bf16)
-    (h_all,) = call(
-        gather_kernel, [shaped((n, rows, width))], (hhat,), [HBM], [HBM], [DMA] + ring_sems(), 2
-    )
-    h_all = h_all.reshape(seq_len, width)
-    gu = jnp.dot(h_all, wcol_all, preferred_element_type=f32)
-    gate, up = gu[:, :ff_mine], gu[:, ff_mine:]
-    sig = jax.nn.sigmoid(gate)
-    active = gate * sig
-    mid = (active * up).astype(bf16)
-    dmid = contract_cols(dy_all, wdown_all)
-    dgate = (dmid * up * sig * (1.0 + gate * (1.0 - sig))).astype(bf16)
-    dup = (dmid * active).astype(bf16)
-    dgu = jnp.concatenate([dgate, dup], axis=-1)
-    part_h = contract_cols(dgu, wcol_all).astype(bf16)
-    part_out = jnp.dot(mid, wdown_all, preferred_element_type=f32).astype(bf16)
-    slot = VMEM((2, n // 2, rows, width), bf16)
-    dweighted, out_sum = call(
-        functools.partial(scatter_kernel, 2),
-        [shaped((rows, width), f32)] * 2,
-        (part_h.reshape(n, rows, width), part_out.reshape(n, rows, width)),
-        [VMEM] * 2,
-        [VMEM] * 2,
-        [slot, slot] + ring_sems() + ring_sems(),
-        3,
+    wdown_all = wdown_all.reshape(ff_mine, width)
+
+    def seq_slots(piece):
+        return [VMEM((2,) + piece, bf16), VMEM((1,) + piece, bf16)]
+
+    slot_shape = VMEM((2, n // 2, rows, width), bf16)
+    col_piece, down_piece = (n * shard, 2 * ff_mine), (ff_own, width)
+    dweighted, out_sum, col_sum, down_sum = call(
+        mlp_kernel,
+        [shaped((rows, width), f32)] * 2 + [shaped(col_piece), shaped(down_piece)],
+        (hhat, dy_all, wcol_all, wdown_all),
+        [HBM] * 4,
+        [VMEM] * 2 + [HBM] * 2,
+        [VMEM((seq_len, width), bf16)] * 2
+        + [VMEM((width, ff_mine), bf16)] * 2
+        + [VMEM((ff_mine, width), bf16)]
+        + [VMEM((seq_len, ff_mine), bf16)] * 3
+        + [VMEM((3 * rows, width), bf16)] * 2
+        + [VMEM((2 * rows, width), bf16)]
+        + [slot_shape] * 2
+        + [VMEM((2,) + col_piece, bf16), VMEM((2,) + col_piece, bf16), VMEM(col_piece, bf16)]
+        + [VMEM((2,) + down_piece, bf16), VMEM((2,) + down_piece, bf16), VMEM(down_piece, bf16)]
+        + [DMA((5,))]
+        + ring_sems() * 3
+        + seq_sems() * 2,
+        2,
     )
     output = (hidden + out_sum).astype(bf16)[None]
 
@@ -845,14 +1084,13 @@
     datt = contract_cols(branch, wout_all).astype(bf16)
     (datt_all,) = call(
         swap_kernel,
-        [shaped((n, rows, head))],
+        [shaped((seq_len, head))],
         (datt.reshape(rows, n, head).transpose(1, 0, 2),),
         [HBM],
         [HBM],
         [DMA] + pair_sems(),
         4,
     )
-    datt_all = datt_all.reshape(seq_len, head)
     dprob = contract_cols(datt_all, v)
     delta = jnp.sum(prob * dprob, axis=-1, keepdims=True)
     dscore = (prob * (dprob - delta)).astype(bf16)
@@ -861,43 +1099,32 @@
     dv = contract_rows(prob_low, datt_all)
     dqkv = jnp.concatenate([dq, dk, dv], axis=-1).astype(bf16)
     part_x = contract_cols(dqkv, wqkv_all).astype(bf16)
-    (xweighted,) = call(
-        functools.partial(scatter_kernel, 1),
-        [shaped((rows, width), f32)],
-        (part_x.reshape(n, rows, width),),
-        [VMEM],
-        [VMEM],
-        [slot] + ring_sems(),
-        5,
-    )
-    grad_tokens = grad_hidden + norm_back(inputs, scale_one, xweighted)
-
-    g_col = contract_rows(h_all, dgu).astype(bf16).reshape(SEQ, n * shard, 2 * ff_mine)
-    g_down = contract_rows(mid, dy_all).astype(bf16).reshape(SEQ, ff_own, width)
     g_qkv = contract_rows(x_all, dqkv).astype(bf16).reshape(SEQ, n * shard, 3 * head)
     g_out = contract_rows(ob_local, branch).astype(bf16).reshape(SEQ, n * shard, width)
-    pieces = (g_col, g_down, g_qkv, g_out)
-    near = []
-    for piece in pieces:
-        near += [VMEM((2,) + piece.shape[1:], bf16), VMEM((1,) + piece.shape[1:], bf16)]
-    col_sum, down_sum, qkv_sum, out_grad = call(
+    xweighted, col_sum, qkv_sum, out_grad = call(
         grads_kernel,
         [
+            shaped((rows, width), f32),
             shaped((n, shard, 2 * ff_mine)),
-            shaped((ff_own, width)),
             shaped((n, shard, 3 * head)),
             shaped((shard, width), f32),
         ],
-        pieces,
-        [VMEM] * 4,
-        [HBM, HBM, HBM, VMEM],
-        near
-        + [VMEM((2, n // 2, shard, width), bf16), DMA((3,))]
-        + seq_sems() * 4
-        + pair_sems() * 2
+        (part_x, col_sum, g_qkv, g_out),
+        [VMEM, HBM, VMEM, VMEM],
+        [VMEM, HBM, HBM, VMEM],
+        [slot_shape]
+        + seq_slots(g_qkv.shape[1:])
+        + seq_slots(g_out.shape[1:])
+        + [VMEM((2, n // 2, shard, width), bf16), DMA((2,))]
+        + ring_sems()
+        + pair_sems()
+        + seq_sems()
+        + pair_sems()
+        + seq_sems()
         + ring_sems(),
-        6,
-    )
+        5,
+    )
+    grad_tokens = grad_hidden + norm_back(inputs, scale_one, xweighted)
     col_sum = col_sum.astype(f32)
 
     def own_columns(t):

time: 877 us -> 655 us (0.75)
  Pallas kernels: 689 us -> 526 us
  matrix products: 108 us -> 43 us
    pallas_call x7 -> x5, Pallas kernels: 689 us -> 526 us  [call(): pl.pallas_call(body, out_shape=outs, in_specs=[pl.BlockSpec(memory_space=...]
    dot_general x6 -> x4, matrix products: 41.3 us -> 17.1 us  [contract_cols(): lax.dot_general(first_mat, second_mat, (((1,), (1,)), ((), ())), preferre...]
    dot_general x2 -> x0, matrix products: 21.3 us -> none  [the longest x1 14.9 us: ring_device(): gu = jnp.dot(h_all, wcol_all, preferred_element_type=f32)]
    dot_general x6 -> x4, matrix products: 31.8 us -> 12.2 us  [contract_rows(): lax.dot_general(first_mat, second_mat, (((0,), (0,)), ((), ())), preferre...]
where the time goes in v2:
time: 655 us; the launch traced here: 645 us
  Pallas kernels  526 us (80%)
  other arithmetic  45.2 us (7%)
  matrix products  43 us (7%)
  local copies, waits for them, and re-layouts  28.9 us (4%)
    pallas_call x5, Pallas kernels, call(): pl.pallas_call(body, out_shape=outs, in_specs=[pl.BlockSpec(memory_space=...  526 us
    dot_general x4, matrix products, contract_cols(): lax.dot_general(first_mat, second_mat, (((1,), (1,)), ((), ())), preferre...  17.1 us

profile of v2, /device:TPU:0, one launch (start us, length us, event | category | flops | bytes accessed | tf_op | source)
XLA Modules:
  0.0 644.8 jit_solution(8897791461915865548)
XLA Ops:
  0.7 0.6 copy-done
  1.3 0.7 convert_element_type.102
  2.0 0.7 convert_element_type.112
  2.6 0.7 compare_select_fusion.2
  3.3 1.2 fusion.7
  4.6 0.6 gather_fusion
  5.2 0.7 subtract_bitcast_fusion
  6.7 1.3 reduce.3
  8.1 0.6 gather_fusion.1
  9.0 1.1 fusion.32
  10.1 1.1 fusion.51
  11.3 0.9 maximum_bitcast_fusion.wqkv
  12.2 0.9 fusion.8.x
  13.1 2.0 fusion.2
  15.8 1.5 stack_reshape.6
  18.1 0.8 stack_reshape.7
  18.8 2.7 pad_maximum_fusion.wcol
  21.6 128.2 %shard_map.221 = (bf16[1024,2048]{1,0:T(8,128)(2,1)}, bf16[4,8,64,768]{3,2,1,0:T(8,128)(2,1)}, bf16[4,8,64,2048]{3,2,1,0:T(8,128)(2,1)}) custom-call(bf16[128,2048]{1,0:T(8,128)(2,1)} %fusion.8.x, bf16[8,64,768]{2,1,0:T(8,128)(2,1)} %maximum_bitcast_fusion.wqkv, bf16[64,2048]{1,0:T(8,128)(2,1)} %wout.1), custom_call_target="tpu_custom_call" | custom-call | tf_op jit(solution)/shard_map/pallas_call | solution.py:636
  149.8 6.2 fusion.71
  156.0 2.4 fusion.35
  158.5 1.2 fusion.70
  159.7 0.6 fusion.1
  160.4 1.3 copy-done.4
  161.7 1.7 convolution_convert_fusion.5.ob
  163.4 114.3 %shard_map.222 = (bf16[8,128,256]{2,1,0:T(8,128)(2,1)}, bf16[1024,2048]{1,0:T(8,128)(2,1)}, bf16[2,4,8,64,1024]{4,3,2,1,0:T(8,128)(2,1)}, bf16[4,256,2048]{2,1,0:T(8,128)(2,1)}) custom-call(bf16[1024,256]{1,0:T(8,128)(2,1)} %convolution_convert_fusion.5.ob, bf16[128,2048]{1,0:T(8,128)(2,1)} %bitcast.117, bf16[2,8,64,1024]{3,2,1,0:T(8,128)(2,1)} %pad_maximum_fusion.wcol, ...), custom_call_target="tpu_custom_call" | custom-call | tf_op jit(solution)/shard_map/pallas_call | solution.py:636
  277.8 1.3 copy.66
  279.1 4.9 multiply_reduce_fusion.2
  284.1 0.9 copy-done.6
  285.1 0.9 multiply_convert_fusion.1.hhat
  286.0 134.6 %shard_map.223 = (f32[128,2048]{1,0:T(8,128)}, f32[128,2048]{1,0:T(8,128)}, bf16[512,2048]{1,0:T(8,128)(2,1)}, bf16[256,2048]{1,0:T(8,128)(2,1)}) custom-call(bf16[128,2048]{1,0:T(8,128)(2,1)} %multiply_convert_fusion.1.hhat, bf16[1024,2048]{1,0:T(8,128)(2,1)} %get-tuple-element.30.dy_hbm, bf16[2,2048,1024]{2,1,0:T(8,128)(2,1)} %bitcast.99, ...), custom_call_target="tpu_custom_call" | custom-call | tf_op jit(solution)/shard_map/pallas_call | solution.py:636
  420.5 1.7 multiply_reduce_fusion.1
  422.3 3.1 subtract_add_fusion
  425.4 6.6 %convolution_convert_fusion.3 = bf16[128,2048]{1,0:T(8,128)(2,1)S(1)} fusion(bf16[2048,2048]{1,0:T(8,128)(2,1)} %bitcast.95, f32[128,2048]{1,0:T(8,128)S(1)} %get-tuple-element.55), kind=kOutput, calls=%fused_computation.16 | convolution fusion | flops 1074266112 | bytes 9961472 | tf_op jit(solution)/shard_map/dot_general | solution.py:65
  432.3 1.0 copy.68
  433.4 14.8 %shard_map.224 = bf16[1024,256]{1,0:T(8,128)(2,1)} custom-call(bf16[8,128,256]{2,1,0:T(8,128)(2,1)} %bitcast.116), custom_call_target="tpu_custom_call" | custom-call | tf_op jit(solution)/shard_map/pallas_call | solution.py:636
  448.2 3.9 multiply_reduce_fusion
  452.1 1.2 multiply_convert_fusion
  453.4 0.7 convolution_multiply_fusion.1
  454.3 0.7 convolution_multiply_fusion
  455.0 2.3 fusion.58
  457.3 2.3 fusion.57
  459.6 2.3 fusion.56
  461.8 2.3 fusion.55
  464.1 1.0 fusion.6
  465.1 1.1 copy-done.28
  466.3 4.9 convolution_convert_fusion.2
  471.2 5.3 convolution_convert_fusion.1.part_x
  476.5 1.5 convert_element_type.127
  478.4 5.5 convolution_convert_fusion
  483.9 134.1 %shard_map.225 = (f32[128,2048]{1,0:T(8,128)}, bf16[8,64,2048]{2,1,0:T(8,128)(2,1)}, bf16[8,64,768]{2,1,0:T(8,128)(2,1)}, f32[64,2048]{1,0:T(8,128)}) custom-call(bf16[1024,2048]{1,0:T(8,128)(2,1)} %convolution_convert_fusion.1.part_x, bf16[512,2048]{1,0:T(8,128)(2,1)} %get-tuple-element.35.col, bf16[4,512,768]{2,1,0:T(8,128)(2,1)} %bitcast.113, ...), custom_call_target="tpu_custom_call" | custom-call | tf_op jit(solution)/shard_map/pallas_call | solution.py:636
  618.1 1.5 fusion.13
  619.6 2.9 fusion.12
  622.9 0.5 copy-done.16
  623.5 1.0 broadcast_multiply_fusion.2
  624.5 1.0 broadcast_multiply_fusion.3
  626.0 2.5 fusion.69
  628.5 2.2 reshape.282
  630.7 1.2 copy.73
  631.9 2.5 copy.83
  634.4 2.5 reshape.280
  636.9 1.2 copy.72
  638.2 1.2 copy.82
  640.3 2.7 broadcast_multiply_fusion
  643.6 0.8 copy.99
  (94 shorter events, 5.9 us)
Async XLA Ops:
  0.6 0.7 copy-start
  0.7 11.5 %copy-start.7 = (bf16[1,128,2048]{2,1,0:T(8,128)(2,1)S(1)}, bf16[1,128,2048]{2,1,0:T(8,128)(2,1)}, u32[]{:S(2)}) copy-start(bf16[1,128,2048]{2,1,0:T(8,128)(2,1)} %param.14) | copy-start | bytes 1572868
  156.0 4.4 copy-start.14
  158.4 1.3 copy-start.22
  158.5 1.3 copy-start.24
  158.5 1.3 copy-start.26
  159.7 2.0 copy-start.4
  279.1 5.0 copy-start.8
  284.1 1.0 copy-start.6
  425.4 6.7 %copy-start.2 = (f32[128,2048]{1,0:T(8,128)}, f32[128,2048]{1,0:T(8,128)S(1)}, u32[]{:S(2)}) copy-start(f32[128,2048]{1,0:T(8,128)S(1)} %get-tuple-element.55) | copy-start | bytes 3145732
  448.2 4.0 copy-start.5
  452.1 1.2 copy-start.25
  452.1 1.2 copy-start.27
  453.3 1.0 copy-start.23
  455.0 9.1 %copy-start.19 = (bf16[1024,256]{1,0:T(8,128)(2,1)S(1)}, bf16[1024,256]{1,0:T(8,128)(2,1)}, u32[]{:S(2)}) copy-start(bf16[1024,256]{1,0:T(8,128)(2,1)} %shard_map.224) | copy-start | bytes 1572868
  464.1 2.2 copy-start.28
  466.3 4.9 copy-start.29
  471.2 5.3 copy-start.15
  476.5 1.6 copy-start.3
  476.5 1.9 copy-start.9
  618.1 4.5 copy-start.17
  622.5 1.0 copy-start.16
  622.7 1.8 copy-start.20
  622.7 1.8 copy-start.21
  622.7 3.3 copy-start.10
  638.1 1.6 copy-start.11
  638.1 1.8 copy-start.12
  638.2 2.1 copy-start.13
  640.3 3.3 copy-start.18
  640.3 4.1 copy-start.1
